TPU v7x, 32 devices: a whole 2x2x4 slice. The times are simulated.
32 devices in a mesh: parts: 2 (over y), seq: 4 (over z), head: 2 (over x), sub: 2 (over core).
Axes of the slice: x: 2, y: 2, z: 4, core: 2. Of those that a mesh axis runs over, the one named last changes fastest.
Arguments:
- ssm_inputs: bfloat16 [4096, 4096], P(('parts', 'seq', 'sub'), 'head'), parts along dimension 0, may hold values from -6 to 6
- gate_inputs: bfloat16 [4096, 4096], P(('parts', 'seq', 'sub'), 'head'), parts along dimension 0, may hold values from -6 to 6
- entry_coeffs: bfloat16 [4096, 128], P(('parts', 'seq', 'sub')), parts along dimension 0, may hold values from -1.796875 to 1.796875
- exit_coeffs: bfloat16 [4096, 128], P(('parts', 'seq', 'sub')), parts along dimension 0, may hold values from -1.796875 to 1.796875
- step_sizes: float32 [32, 4096], P('head', ('parts', 'seq', 'sub')), parts along dimension 1, may hold values from 0.01 to 0.12
- log_rates: float32 [32], P('head'), may hold values from -11 to 0
- skip_gains: float32 [32], P('head'), may hold values from 0.8 to 11.25
- norm_gains: float32 [4096], P('head'), may hold values from 0.1 to 1.9
- mixer_grad: bfloat16 [4096, 4096], P(('parts', 'seq', 'sub'), 'head'), parts along dimension 0, may hold values from -6 to 6
- queries: bfloat16 [4096, 2048], P(('parts', 'seq', 'sub'), 'head'), parts along dimension 0, may hold values from -6 to 6
- key_rows: bfloat16 [4096, 2048], P(('parts', 'seq', 'sub'), 'head'), parts along dimension 0, may hold values from -6 to 6
- value_rows: bfloat16 [4096, 2048], P(('parts', 'seq', 'sub'), 'head'), parts along dimension 0, may hold values from -6 to 6
- attention_grad: bfloat16 [4096, 2048], P(('parts', 'seq', 'sub'), 'head'), parts along dimension 0, may hold values from -6 to 6
Outputs:
- grad_inputs: bfloat16 [4096, 4096], P(('parts', 'seq', 'sub'), 'head'), parts along dimension 0
- grad_entry: bfloat16 [4096, 128], P(('parts', 'seq', 'sub')), parts along dimension 0
- grad_exit: bfloat16 [4096, 128], P(('parts', 'seq', 'sub')), parts along dimension 0
- grad_steps: float32 [32, 4096], P('head', ('parts', 'seq', 'sub')), parts along dimension 1
- grad_rates: float32 [64], P(('parts', 'head')), parts along dimension 0
- grad_skip: float32 [64], P(('parts', 'head')), parts along dimension 0
- grad_gains: float32 [8192], P(('parts', 'head')), parts along dimension 0
- grad_queries: bfloat16 [4096, 2048], P(('parts', 'seq', 'sub'), 'head'), parts along dimension 0
- grad_keys: bfloat16 [4096, 2048], P(('parts', 'seq', 'sub'), 'head'), parts along dimension 0
- grad_values: bfloat16 [4096, 2048], P(('parts', 'seq', 'sub'), 'head'), parts along dimension 0
There are 2 independent parts, one for each index of `parts`. A program takes and returns all parts, laid end to end along the dimension named above; an argument that names none is the same for every part. Nothing has to cross between parts.
All inputs are finite; a program needn't handle non-finite values.
Results may differ from a plain program's by a relative error of at most 0.012.
The roundings to bfloat16 on the way count: a program that leaves them out, or rounds other values in their place, can miss the bound.
Values may be sent and summed in bfloat16 or wider, within the bound.
No kernel may reach another device: no remote copies, remote signals or barrier semaphores. Data moves between devices by JAX's collectives and lax.ppermute only.
A program may use at most 192 MiB of HBM per device.

v0:
```python
import jax
import jax.numpy as jnp
from jax import lax
from jax.sharding import PartitionSpec as P

HP = 128
AD = 128
W = 2048
DI = 4096


EPSILON = 1e-05
HIGHEST_PRECISION = lax.Precision.HIGHEST


def carried_in(part, axis, combine, identity, reverse):
    count = lax.axis_size(axis)
    place = lax.axis_index(axis)
    ahead = count - 1 - place if reverse else place
    gathered = jax.tree.map(lambda a: lax.all_gather(a, axis), part)
    state = jax.tree.map(lambda a, e: jnp.zeros_like(a) + jnp.asarray(e, a.dtype), part, identity)

    def one(step, state):
        source = count - 1 - step if reverse else step
        return combine(
            state, jax.tree.map(lambda a: lax.dynamic_index_in_dim(a, source, 0, False), gathered)
        )

    return lax.fori_loop(0, ahead, one, state)


def passed_along(value, axis, steps):
    count = lax.axis_size(axis)
    first, last = (max(0, -steps), min(count, count - steps))
    return lax.ppermute(value, axis, [(source, source + steps) for source in range(first, last)])


def decay_logs(block_steps, log_rates):
    return jnp.cumsum(-jnp.exp(log_rates)[:, None] * block_steps, axis=1)


def group_states(inputs_heads, entry_wide, block_steps, log_rates):
    cumulative = decay_logs(block_steps, log_rates)
    tail_decay = jnp.exp(cumulative[:, -1:] - cumulative)
    weighted = inputs_heads * (block_steps * tail_decay).T[:, :, None]
    states = jnp.einsum("tn,thp->hnp", entry_wide, weighted, precision=HIGHEST_PRECISION)
    return (jnp.exp(cumulative[:, -1]), states)


def ssd_block(
    inputs_heads, gram_matrix, entry_wide, exit_wide, block_steps, log_rates, start_state
):
    block_rows = inputs_heads.shape[0]
    cumulative = decay_logs(block_steps, log_rates)
    positions = jnp.arange(block_rows, dtype=jnp.int32)
    causal = (positions[:, None] >= positions[None, :])[None]
    spread_log = cumulative[:, :, None] - cumulative[:, None, :]
    decay_matrix = jnp.where(causal, jnp.exp(jnp.where(causal, spread_log, 0.0)), 0.0)
    scaled_in = inputs_heads * block_steps.T[:, :, None]
    within_block = jnp.einsum(
        "hts,shp->thp", gram_matrix[None] * decay_matrix, scaled_in, precision=HIGHEST_PRECISION
    )
    carried = (
        jnp.einsum("tn,hnp->thp", exit_wide, start_state, precision=HIGHEST_PRECISION)
        * jnp.exp(cumulative).T[:, :, None]
    )
    tail_decay = jnp.exp(cumulative[:, -1:] - cumulative)
    final_state = jnp.exp(cumulative[:, -1])[:, None, None] * start_state + jnp.einsum(
        "tn,thp->hnp", entry_wide, scaled_in * tail_decay.T[:, :, None], precision=HIGHEST_PRECISION
    )
    return (within_block + carried, final_state)


def chain_combine(earlier, later):
    return (earlier[0] * later[0], later[0][:, None, None] * earlier[1] + later[1])


def window_grads(query_block, key_block, value_block, grad_block, query_pos, key_pos):
    score_scale = AD ** (-0.5)
    query_heads = query_block.reshape(query_block.shape[0], -1, AD)
    key_heads = key_block.reshape(key_block.shape[0], -1, AD)
    value_heads = value_block.reshape(value_block.shape[0], -1, AD)
    grad_heads = grad_block.reshape(grad_block.shape[0], -1, AD)
    scores = (
        jnp.einsum("thd,khd->htk", query_heads, key_heads, preferred_element_type=jnp.float32)
        * score_scale
    )
    gaps = query_pos[:, None] - key_pos[None, :]
    valid = (gaps >= 0) & (gaps < W) & (key_pos[None, :] >= 0)
    scores = jnp.where(valid[None], scores, -1e30)
    top_score = jnp.max(scores, axis=-1, keepdims=True)
    expos = jnp.exp(scores - top_score)
    probs = expos / jnp.sum(expos, axis=-1, keepdims=True)
    probs_low = probs.astype(jnp.bfloat16)
    attended = jnp.einsum(
        "htk,khd->thd", probs_low, value_heads, preferred_element_type=jnp.float32
    )
    delta = jnp.sum(grad_heads.astype(jnp.float32) * attended, axis=-1).T
    dprobs = jnp.einsum("thd,khd->htk", grad_heads, value_heads, preferred_element_type=jnp.float32)
    dscores_low = (probs * (dprobs - delta[:, :, None]) * score_scale).astype(jnp.bfloat16)
    grad_query = jnp.einsum(
        "htk,khd->thd", dscores_low, key_heads, preferred_element_type=jnp.float32
    )
    grad_key = jnp.einsum(
        "htk,thd->khd", dscores_low, query_heads, preferred_element_type=jnp.float32
    )
    grad_value = jnp.einsum(
        "htk,thd->khd", probs_low, grad_heads, preferred_element_type=jnp.float32
    )
    return (grad_query, grad_key, grad_value)


def on_device(
    ssm_inputs,
    gate_inputs,
    entry_coeffs,
    exit_coeffs,
    step_sizes,
    log_rates,
    skip_gains,
    norm_gains,
    mixer_grad,
    queries,
    key_rows,
    value_rows,
    attention_grad,
):
    shard_rows = ssm_inputs.shape[0]
    local_heads = log_rates.shape[0]
    inputs_heads = ssm_inputs.astype(jnp.float32).reshape(shard_rows, local_heads, HP)
    entry_wide = entry_coeffs.astype(jnp.float32)
    exit_wide = exit_coeffs.astype(jnp.float32)
    gram_matrix = jnp.dot(exit_coeffs, entry_coeffs.T, preferred_element_type=jnp.float32)
    decay_total, local_state = group_states(inputs_heads, entry_wide, step_sizes, log_rates)
    identity = (jnp.ones((local_heads,), jnp.float32), jnp.zeros_like(local_state))
    start_state = carried_in(
        (decay_total, local_state), ("seq", "sub"), chain_combine, identity, False
    )[1]
    (ssd_out, final_state), pullback = jax.vjp(
        ssd_block,
        inputs_heads,
        gram_matrix,
        entry_wide,
        exit_wide,
        step_sizes,
        log_rates,
        start_state,
    )
    mixed = (ssd_out + skip_gains[None, :, None] * inputs_heads).reshape(shard_rows, -1)
    silu_gate = jax.nn.silu(gate_inputs.astype(jnp.float32))
    gated = mixed * silu_gate
    square_sum = lax.psum(jnp.sum(gated * gated, axis=1), "head")
    inv_rms = lax.rsqrt(square_sum / DI + EPSILON)
    grad_wide = mixer_grad.astype(jnp.float32)
    gain_local = jnp.sum(grad_wide * gated * inv_rms[:, None], axis=0)
    cross_sum = lax.psum(jnp.sum(grad_wide * norm_gains[None] * gated, axis=1), "head")
    grad_gated = (
        inv_rms[:, None] * norm_gains[None] * grad_wide
        - gated * (inv_rms**3 * cross_sum / DI)[:, None]
    )
    grad_mixed = (grad_gated * silu_gate).reshape(shard_rows, local_heads, HP)
    skip_local = jnp.sum(grad_mixed * inputs_heads, axis=(0, 2))
    cumulative = decay_logs(step_sizes, log_rates)
    local_pull = jnp.einsum(
        "tn,thp->hnp",
        exit_wide,
        grad_mixed * jnp.exp(cumulative).T[:, :, None],
        precision=HIGHEST_PRECISION,
    )
    later_pull = carried_in(
        (decay_total, local_pull), ("seq", "sub"), chain_combine, identity, True
    )[1]
    grads = pullback((grad_mixed, later_pull))
    grad_gram = grads[1]
    entry_sum = grads[2] + jnp.dot(grad_gram.T, exit_wide, precision=HIGHEST_PRECISION)
    exit_sum = grads[3] + jnp.dot(grad_gram, entry_wide, precision=HIGHEST_PRECISION)
    grad_inputs = (
        (grads[0] + skip_gains[None, :, None] * grad_mixed)
        .reshape(shard_rows, -1)
        .astype(jnp.bfloat16)
    )
    grad_entry, grad_exit = lax.psum((entry_sum, exit_sum), "head")
    grad_rates, grad_skip, grad_gains = lax.psum((grads[5], skip_local, gain_local), ("seq", "sub"))
    reach_shards = W // shard_rows
    first_row = lax.axis_index(("seq", "sub")) * shard_rows
    key_parts = []
    value_parts = []
    for shift_by in range(reach_shards, 0, -1):
        arrived = passed_along((key_rows, value_rows), ("seq", "sub"), shift_by)
        key_parts.append(arrived[0])
        value_parts.append(arrived[1])
    key_window = jnp.concatenate(key_parts + [key_rows], axis=0)
    value_window = jnp.concatenate(value_parts + [value_rows], axis=0)
    query_pos = first_row + jnp.arange(shard_rows, dtype=jnp.int32)
    key_pos = (
        first_row
        - reach_shards * shard_rows
        + jnp.arange((reach_shards + 1) * shard_rows, dtype=jnp.int32)
    )
    grad_query, grad_key, grad_value = window_grads(
        queries, key_window, value_window, attention_grad, query_pos, key_pos
    )
    key_terms = grad_key.reshape(grad_key.shape[0], -1)
    value_terms = grad_value.reshape(grad_value.shape[0], -1)
    key_total = key_terms[reach_shards * shard_rows :]
    value_total = value_terms[reach_shards * shard_rows :]
    for shift_by in range(1, reach_shards + 1):
        low_row = (reach_shards - shift_by) * shard_rows
        arrived = passed_along(
            (
                key_terms[low_row : low_row + shard_rows],
                value_terms[low_row : low_row + shard_rows],
            ),
            ("seq", "sub"),
            -shift_by,
        )
        key_total = key_total + arrived[0]
        value_total = value_total + arrived[1]
    return (
        grad_inputs,
        grad_entry.astype(jnp.bfloat16),
        grad_exit.astype(jnp.bfloat16),
        grads[4],
        grad_rates,
        grad_skip,
        grad_gains,
        grad_query.reshape(shard_rows, -1).astype(jnp.bfloat16),
        key_total.astype(jnp.bfloat16),
        value_total.astype(jnp.bfloat16),
    )


def solution(mesh):
    in_specs = (
        P(("parts", "seq", "sub"), "head"),
        P(("parts", "seq", "sub"), "head"),
        P(("parts", "seq", "sub"), None),
        P(("parts", "seq", "sub"), None),
        P("head", ("parts", "seq", "sub")),
        P("head"),
        P("head"),
        P("head"),
        P(("parts", "seq", "sub"), "head"),
        P(("parts", "seq", "sub"), "head"),
        P(("parts", "seq", "sub"), "head"),
        P(("parts", "seq", "sub"), "head"),
        P(("parts", "seq", "sub"), "head"),
    )
    out_specs = (
        P(("parts", "seq", "sub"), "head"),
        P(("parts", "seq", "sub"), None),
        P(("parts", "seq", "sub"), None),
        P("head", ("parts", "seq", "sub")),
        P(("parts", "head")),
        P(("parts", "head")),
        P(("parts", "head")),
        P(("parts", "seq", "sub"), "head"),
        P(("parts", "seq", "sub"), "head"),
        P(("parts", "seq", "sub"), "head"),
    )
    return jax.shard_map(
        on_device, mesh=mesh, in_specs=in_specs, out_specs=out_specs, check_vma=False
    )
```

profile of v0, /device:TPU:0, one launch (start us, length us, event | category | flops | bytes accessed | tf_op | source)
XLA Modules:
  0.0 845.3 jit_solution(189986210536674276)
XLA Ops:
  36.1 79.2 %all-reduce.2 = f32[128]{0:T(128)S(1)} all-reduce(f32[128]{0:T(128)S(1)} %dynamic-update-slice), channel_id=2, replica_groups=mesh['parts'=2,'seq'=4,'head'=2,'sub'=2] {'seq','sub'}, use_global_device_ids=true, to_apply=%add.2 | all-reduce | flops 128 | bytes 1024
  140.8 18.4 %collective-permute-start.9 = (bf16[256,1024]{0,1:T(8,128)(2,1)S(1)}, bf16[256,1024]{0,1:T(8,128)(2,1)S(1)}, u32[]{:S(2)}, u32[]{:S(2)}) collective-permute-start(bf16[256,1024]{0,1:T(8,128)(2,1)S(1)} %copy.300), channel_id=1, source_target_pairs={{0,13},{2,15},{16,29},{18,31}} | collective-permute-start | bytes 1572872 | tf_op jit(solution)/shard_map/ppermute | solution.py:35
  159.2 17.5 %collective-permute-start.10 = (bf16[256,1024]{0,1:T(8,128)(2,1)S(1)}, bf16[256,1024]{0,1:T(8,128)(2,1)S(1)}, u32[]{:S(2)}, u32[]{:S(2)}) collective-permute-start(bf16[256,1024]{0,1:T(8,128)(2,1)S(1)} %copy.300), channel_id=1, source_target_pairs={{0,12},{1,13},{2,14},{3,15},{16,28},{17,29},{18,30},{19,31}} | collective-permute-start | bytes 1572872 | tf_op jit(solution)/shard_map/ppermute | solution.py:35
  176.8 33.5 %collective-permute-start.11 = (bf16[256,1024]{0,1:T(8,128)(2,1)S(1)}, bf16[256,1024]{0,1:T(8,128)(2,1)S(1)}, u32[]{:S(2)}, u32[]{:S(2)}) collective-permute-start(bf16[256,1024]{0,1:T(8,128)(2,1)S(1)} %copy.300), channel_id=1, source_target_pairs={{0,9},{1,12},{4,13},{2,11},{3,14},{6,15},{16,25},{17,28},{20,29},{... | collective-permute-start | bytes 1572872 | tf_op jit(solution)/shard_map/ppermute | solution.py:35
  210.4 14.9 %collective-permute-start.13 = (bf16[256,1024]{0,1:T(8,128)(2,1)S(1)}, bf16[256,1024]{0,1:T(8,128)(2,1)S(1)}, u32[]{:S(2)}, u32[]{:S(2)}) collective-permute-start(bf16[256,1024]{0,1:T(8,128)(2,1)S(1)} %copy.300), channel_id=1, source_target_pairs={{0,5},{1,8},{4,9},{5,12},{8,13},{2,7},{3,10},{6,11},{7,14},{10,15}... | collective-permute-start | bytes 1572872 | tf_op jit(solution)/shard_map/ppermute | solution.py:35
  236.8 10.4 %collective-permute-done.14 = bf16[256,1024]{0,1:T(8,128)(2,1)S(1)} collective-permute-done((bf16[256,1024]{0,1:T(8,128)(2,1)S(1)}, bf16[256,1024]{0,1:T(8,128)(2,1)S(1)}, u32[]{:S(2)}, u32[]{:S(2)}) %collective-permute-start.14) | collective-permute-done | bytes 524320 | tf_op jit(solution)/shard_map/ppermute | solution.py:35
  251.0 7.8 fusion.31
  294.0 12.4 %fusion.111 = (f32[8,256]{1,0:T(8,128)S(1)}, f32[8,256,2304]{1,2,0:T(8,128)}) fusion(pred[256,2304]{0,1:T(8,128)(4,1)} %fusion.19, bf16[2304,8,128]{0,2,1:T(8,128)(2,1)} %bitcast.228, bf16[256,8,128]{0,2,1:T(8,128)(2,1)} %bitcast.254), kind=kOutput, calls=%fused_computation.172 | convolution fusion | flops 1226836224 | bytes 24715264 | tf_op jit(solution)/shard_map/sub | solution.py:92
  306.4 7.7 fusion.7
  321.3 13.0 %fusion.2 = bf16[8,256,2304]{1,2,0:T(8,128)(2,1)} fusion(bf16[2304,8,128]{0,2,1:T(8,128)(2,1)} %bitcast.36, bf16[256,8,128]{0,2,1:T(8,128)(2,1)S(1)} %bitcast.232, f32[8,256]{1,0:T(8,128)S(1)} %bitcast.262, f32[8,256,2304]{1,2,0:T(8,128)} %get-tuple-element.284, f32[8,256]{1,0:T(8,128)S(1)} %get-tuple-element.283), kind=kOutput, calls=%fused_computation.7 | convolution fusion | flops 1231552512 | bytes 33570816 | tf_op jit(solution)/shard_map/thd,khd->htk/dot_general | solution.py:99
  334.3 10.5 %convolution_bitcast_fusion.1 = f32[2304,8,128]{0,2,1:T(8,128)} fusion(bf16[8,256,2304]{1,2,0:T(8,128)(2,1)} %fusion.2, bf16[256,8,128]{0,2,1:T(8,128)(2,1)S(1)} %bitcast.255), kind=kOutput, calls=%fused_computation.17 | convolution fusion | flops 1207959552 | bytes 19398656 | tf_op jit(solution)/shard_map/htk,thd->khd/dot_general | solution.py:104
  344.8 7.5 fusion.110
  356.1 10.5 %convolution_bitcast_fusion = f32[2304,8,128]{0,2,1:T(8,128)} fusion(bf16[8,256,2304]{1,2,0:T(8,128)(2,1)} %copy-done.1, bf16[256,8,128]{0,2,1:T(8,128)(2,1)} %bitcast.230), kind=kOutput, calls=%fused_computation.16 | convolution fusion | flops 1207959552 | bytes 19398656 | tf_op jit(solution)/shard_map/htk,thd->khd/dot_general | solution.py:107
  366.7 7.5 fusion.109
  392.2 31.7 %collective-permute-done.17 = f32[256,1024]{1,0:T(8,128)} collective-permute-done((f32[256,1024]{1,0:T(8,128)}, f32[256,1024]{1,0:T(8,128)}, u32[]{:S(2)}, u32[]{:S(2)}) %collective-permute-start.17) | collective-permute-done | bytes 1048608 | tf_op jit(solution)/shard_map/ppermute | solution.py:35
  438.1 13.6 %collective-permute-done.18 = f32[256,1024]{1,0:T(8,128)} collective-permute-done((f32[256,1024]{1,0:T(8,128)}, f32[256,1024]{1,0:T(8,128)}, u32[]{:S(2)}, u32[]{:S(2)}) %collective-permute-start.18) | collective-permute-done | bytes 1048608 | tf_op jit(solution)/shard_map/ppermute | solution.py:35
  453.0 120.1 %collective-permute-done.19 = f32[256,1024]{1,0:T(8,128)} collective-permute-done((f32[256,1024]{1,0:T(8,128)}, f32[256,1024]{1,0:T(8,128)}, u32[]{:S(2)}, u32[]{:S(2)}) %collective-permute-start.19) | collective-permute-done | bytes 1048608 | tf_op jit(solution)/shard_map/ppermute | solution.py:35
  577.3 85.6 %collective-permute-done.27 = f32[256,1024]{1,0:T(8,128)} collective-permute-done((f32[256,1024]{1,0:T(8,128)}, f32[256,1024]{1,0:T(8,128)}, u32[]{:S(2)}, u32[]{:S(2)}) %collective-permute-start.27) | collective-permute-done | bytes 1048608 | tf_op jit(solution)/shard_map/ppermute | solution.py:35
  686.9 7.3 convolution_convert_fusion
  706.9 51.9 %collective-permute-done.20 = f32[256,1024]{1,0:T(8,128)} collective-permute-done((f32[256,1024]{1,0:T(8,128)}, f32[256,1024]{1,0:T(8,128)}, u32[]{:S(2)}, u32[]{:S(2)}) %collective-permute-start.20) | collective-permute-done | bytes 1048608 | tf_op jit(solution)/shard_map/ppermute | solution.py:35
  775.0 15.4 %while.27 = (s32[]{:T(128)}, f32[16,128,128]{2,1,0:T(8,128)S(1)}, s32[]{:T(128)}, f32[8,16]{1,0:T(8,128)}, f32[8,16,128,128]{3,2,1,0:T(8,128)}, /*index=5*/s32[]{:T(128)}, s32[]{:T(128)}, s32[]{:T(128)}, s32[]{:T(128)}) while((s32[]{:T(128)}, f32[16,128,128]{2,1,0:T(8,128)S(1)}, s32[]{:T(128)}, f32[8,16]{1,0:T(8,128)}, ...), condition=%wide.region_9.10_spmd, body=%wide.region_8.9_spmd.sunk | while | flops 524294 | bytes 3146075 | solution.py:29
  798.8 7.5 fusion.29
  811.5 11.8 %all-reduce.6 = (bf16[256,128]{1,0:T(8,128)(2,1)}, bf16[256,128]{1,0:T(8,128)(2,1)}) all-reduce(f32[256,128]{1,0:T(8,128)S(1)} %convolution_add_fusion.1, f32[256,128]{1,0:T(8,128)S(1)} %convolution_add_fusion), channel_id=1, replica_groups=mesh['parts'=2,'seq'=4,'head'=2,'sub'=2] {'head'}, use_global_device_ids=true, to_apply=%region_11.12 | all-reduce | flops 65536 | bytes 393216 | tf_op jit(solution)/shard_map/psum | solution.py:182
  823.3 14.7 %all-reduce.3 = (f32[16]{0:T(128)}, f32[16]{0:T(128)}, f32[2048]{0:T(1024)}) all-reduce(f32[16]{0:T(128)S(1)} %negate_multiply_fusion, f32[16]{0:T(128)S(1)} %bitcast_reduce_fusion, f32[2048]{0:T(1024)S(1)} %copy-done.22), channel_id=1, replica_groups=mesh['parts'=2,'seq'=4,'head'=2,'sub'=2] {'seq','sub'}, use_global_device_ids=true, to_apply=%region_23.24 | all-reduce | flops 2080 | bytes 16640 | tf_op jit(solution)/shard_map/psum | solution.py:183
  (251 shorter events, 233.8 us)
Async XLA Ops:
  7.2 242.6 %all-gather.6.cloned.1.call-start = ((), (), s32[]{:S(2)}) async-start(), calls=%async_computation | async-start | bytes 9437184 | tf_op jit(solution)/shard_map/all_gather | solution.py:20
  15.2 759.8 %all-gather.8.cloned.1.call-start = ((), (), s32[]{:S(2)}) async-start(), calls=%async_computation.1 | async-start | bytes 9437184 | tf_op jit(solution)/shard_map/all_gather | solution.py:20
  16.5 116.4 %collective-permute-start.4 = (bf16[256,1024]{0,1:T(8,128)(2,1)S(1)}, bf16[256,1024]{0,1:T(8,128)(2,1)}, u32[]{:S(2)}, u32[]{:S(2)}) collective-permute-start(bf16[256,1024]{0,1:T(8,128)(2,1)S(1)} %copy.289), channel_id=1, source_target_pairs={{0,8},{1,9},{4,12},{5,13},{2,10},{3,11},{6,14},{7,15},{16,24},{17,... | collective-permute-start | bytes 1572872 | tf_op jit(solution)/shard_map/ppermute | solution.py:35
  23.3 106.5 %collective-permute-start.3 = (bf16[256,1024]{0,1:T(8,128)(2,1)S(1)}, bf16[256,1024]{0,1:T(8,128)(2,1)}, u32[]{:S(2)}, u32[]{:S(2)}) collective-permute-start(bf16[256,1024]{0,1:T(8,128)(2,1)S(1)} %copy.289), channel_id=1, source_target_pairs={{0,9},{1,12},{4,13},{2,11},{3,14},{6,15},{16,25},{17,28},{20,29},{... | collective-permute-start | bytes 1572872 | tf_op jit(solution)/shard_map/ppermute | solution.py:35
  25.4 101.9 %collective-permute-start.2 = (bf16[256,1024]{0,1:T(8,128)(2,1)S(1)}, bf16[256,1024]{0,1:T(8,128)(2,1)}, u32[]{:S(2)}, u32[]{:S(2)}) collective-permute-start(bf16[256,1024]{0,1:T(8,128)(2,1)S(1)} %copy.289), channel_id=1, source_target_pairs={{0,12},{1,13},{2,14},{3,15},{16,28},{17,29},{18,30},{19,31}} | collective-permute-start | bytes 1572872 | tf_op jit(solution)/shard_map/ppermute | solution.py:35
  27.5 95.6 %collective-permute-start.1 = (bf16[256,1024]{0,1:T(8,128)(2,1)S(1)}, bf16[256,1024]{0,1:T(8,128)(2,1)}, u32[]{:S(2)}, u32[]{:S(2)}) collective-permute-start(bf16[256,1024]{0,1:T(8,128)(2,1)S(1)} %copy.289), channel_id=1, source_target_pairs={{0,13},{2,15},{16,29},{18,31}} | collective-permute-start | bytes 1572872 | tf_op jit(solution)/shard_map/ppermute | solution.py:35
  29.6 91.2 %collective-permute-start = (bf16[256,1024]{0,1:T(8,128)(2,1)S(1)}, bf16[256,1024]{0,1:T(8,128)(2,1)}, u32[]{:S(2)}, u32[]{:S(2)}) collective-permute-start(bf16[256,1024]{0,1:T(8,128)(2,1)S(1)} %copy.289), channel_id=1, source_target_pairs={} | collective-permute-start | bytes 1572872 | tf_op jit(solution)/shard_map/ppermute | solution.py:35
  129.8 104.6 %collective-permute-start.12 = (bf16[256,1024]{0,1:T(8,128)(2,1)S(1)}, bf16[256,1024]{0,1:T(8,128)(2,1)S(1)}, u32[]{:S(2)}, u32[]{:S(2)}) collective-permute-start(bf16[256,1024]{0,1:T(8,128)(2,1)S(1)} %copy.300), channel_id=1, source_target_pairs={{0,8},{1,9},{4,12},{5,13},{2,10},{3,11},{6,14},{7,15},{16,24},{17,... | collective-permute-start | bytes 1572872 | tf_op jit(solution)/shard_map/ppermute | solution.py:35
  132.9 77.5 %collective-permute-start.8 = (bf16[256,1024]{0,1:T(8,128)(2,1)S(1)}, bf16[256,1024]{0,1:T(8,128)(2,1)S(1)}, u32[]{:S(2)}, u32[]{:S(2)}) collective-permute-start(bf16[256,1024]{0,1:T(8,128)(2,1)S(1)} %copy.300), channel_id=1, source_target_pairs={} | collective-permute-start | bytes 1572872 | tf_op jit(solution)/shard_map/ppermute | solution.py:35
  140.8 85.4 %collective-permute-start.9 = (bf16[256,1024]{0,1:T(8,128)(2,1)S(1)}, bf16[256,1024]{0,1:T(8,128)(2,1)S(1)}, u32[]{:S(2)}, u32[]{:S(2)}) collective-permute-start(bf16[256,1024]{0,1:T(8,128)(2,1)S(1)} %copy.300), channel_id=1, source_target_pairs={{0,13},{2,15},{16,29},{18,31}} | collective-permute-start | bytes 1572872 | tf_op jit(solution)/shard_map/ppermute | solution.py:35
  159.2 69.1 %collective-permute-start.10 = (bf16[256,1024]{0,1:T(8,128)(2,1)S(1)}, bf16[256,1024]{0,1:T(8,128)(2,1)S(1)}, u32[]{:S(2)}, u32[]{:S(2)}) collective-permute-start(bf16[256,1024]{0,1:T(8,128)(2,1)S(1)} %copy.300), channel_id=1, source_target_pairs={{0,12},{1,13},{2,14},{3,15},{16,28},{17,29},{18,30},{19,31}} | collective-permute-start | bytes 1572872 | tf_op jit(solution)/shard_map/ppermute | solution.py:35
  385.8 187.2 %collective-permute-start.19 = (f32[256,1024]{1,0:T(8,128)}, f32[256,1024]{1,0:T(8,128)}, u32[]{:S(2)}, u32[]{:S(2)}) collective-permute-start(f32[256,1024]{1,0:T(8,128)} %copy.320), channel_id=1, source_target_pairs={{8,0},{9,1},{12,4},{13,5},{10,2},{11,3},{14,6},{15,7},{24,16},{25,... | collective-permute-start | bytes 3145736 | tf_op jit(solution)/shard_map/ppermute | solution.py:35
  387.1 187.2 %collective-permute-start.25 = (f32[256,1024]{1,0:T(8,128)}, f32[256,1024]{1,0:T(8,128)}, u32[]{:S(2)}, u32[]{:S(2)}) collective-permute-start(f32[256,1024]{1,0:T(8,128)} %copy.328), channel_id=1, source_target_pairs={{4,0},{5,1},{8,4},{9,5},{12,8},{13,9},{6,2},{7,3},{10,6},{11,7},{1... | collective-permute-start | bytes 3145736 | tf_op jit(solution)/shard_map/ppermute | solution.py:35
  390.9 184.7 %collective-permute-start.26 = (f32[256,1024]{1,0:T(8,128)}, f32[256,1024]{1,0:T(8,128)}, u32[]{:S(2)}, u32[]{:S(2)}) collective-permute-start(f32[256,1024]{1,0:T(8,128)} %copy.329), channel_id=1, source_target_pairs={{5,0},{8,1},{9,4},{12,5},{13,8},{7,2},{10,3},{11,6},{14,7},{15,10}... | collective-permute-start | bytes 3145736 | tf_op jit(solution)/shard_map/ppermute | solution.py:35
  423.9 239.0 %collective-permute-start.27 = (f32[256,1024]{1,0:T(8,128)}, f32[256,1024]{1,0:T(8,128)}, u32[]{:S(2)}, u32[]{:S(2)}) collective-permute-start(f32[256,1024]{1,0:T(8,128)} %copy.330), channel_id=1, source_target_pairs={{8,0},{9,1},{12,4},{13,5},{10,2},{11,3},{14,6},{15,7},{24,16},{25,... | collective-permute-start | bytes 3145736 | tf_op jit(solution)/shard_map/ppermute | solution.py:35
  451.7 228.1 %collective-permute-start.28 = (f32[256,1024]{1,0:T(8,128)}, f32[256,1024]{1,0:T(8,128)}, u32[]{:S(2)}, u32[]{:S(2)}) collective-permute-start(f32[256,1024]{1,0:T(8,128)} %copy.331), channel_id=1, source_target_pairs={{9,0},{12,1},{13,4},{11,2},{14,3},{15,6},{25,16},{28,17},{29,20},{... | collective-permute-start | bytes 3145736 | tf_op jit(solution)/shard_map/ppermute | solution.py:35
  573.0 108.1 %collective-permute-start.29 = (f32[256,1024]{1,0:T(8,128)}, f32[256,1024]{1,0:T(8,128)}, u32[]{:S(2)}, u32[]{:S(2)}) collective-permute-start(f32[256,1024]{1,0:T(8,128)} %copy.332), channel_id=1, source_target_pairs={{12,0},{13,1},{14,2},{15,3},{28,16},{29,17},{30,18},{31,19}} | collective-permute-start | bytes 3145736 | tf_op jit(solution)/shard_map/ppermute | solution.py:35
  574.3 108.1 %collective-permute-start.30 = (f32[256,1024]{1,0:T(8,128)}, f32[256,1024]{1,0:T(8,128)}, u32[]{:S(2)}, u32[]{:S(2)}) collective-permute-start(f32[256,1024]{1,0:T(8,128)} %copy.333), channel_id=1, source_target_pairs={{13,0},{15,2},{29,16},{31,18}} | collective-permute-start | bytes 3145736 | tf_op jit(solution)/shard_map/ppermute | solution.py:35
  575.6 108.1 %collective-permute-start.31 = (f32[256,1024]{1,0:T(8,128)}, f32[256,1024]{1,0:T(8,128)}, u32[]{:S(2)}, u32[]{:S(2)}) collective-permute-start(f32[256,1024]{1,0:T(8,128)} %copy.334), channel_id=1, source_target_pairs={} | collective-permute-start | bytes 3145736 | tf_op jit(solution)/shard_map/ppermute | solution.py:35
  679.8 78.9 %collective-permute-start.20 = (f32[256,1024]{1,0:T(8,128)}, f32[256,1024]{1,0:T(8,128)}, u32[]{:S(2)}, u32[]{:S(2)}) collective-permute-start(f32[256,1024]{1,0:T(8,128)} %copy.321), channel_id=1, source_target_pairs={{9,0},{12,1},{13,4},{11,2},{14,3},{15,6},{25,16},{28,17},{29,20},{... | collective-permute-start | bytes 3145736 | tf_op jit(solution)/shard_map/ppermute | solution.py:35
  681.1 77.6 %collective-permute-start.21 = (f32[256,1024]{1,0:T(8,128)}, f32[256,1024]{1,0:T(8,128)}, u32[]{:S(2)}, u32[]{:S(2)}) collective-permute-start(f32[256,1024]{1,0:T(8,128)} %copy.322), channel_id=1, source_target_pairs={{12,0},{13,1},{14,2},{15,3},{28,16},{29,17},{30,18},{31,19}} | collective-permute-start | bytes 3145736 | tf_op jit(solution)/shard_map/ppermute | solution.py:35
  682.4 76.3 %collective-permute-start.22 = (f32[256,1024]{1,0:T(8,128)}, f32[256,1024]{1,0:T(8,128)}, u32[]{:S(2)}, u32[]{:S(2)}) collective-permute-start(f32[256,1024]{1,0:T(8,128)} %copy.323), channel_id=1, source_target_pairs={{13,0},{15,2},{29,16},{31,18}} | collective-permute-start | bytes 3145736 | tf_op jit(solution)/shard_map/ppermute | solution.py:35
  683.7 75.0 %collective-permute-start.23 = (f32[256,1024]{1,0:T(8,128)}, f32[256,1024]{1,0:T(8,128)}, u32[]{:S(2)}, u32[]{:S(2)}) collective-permute-start(f32[256,1024]{1,0:T(8,128)} %copy.324), channel_id=1, source_target_pairs={} | collective-permute-start | bytes 3145736 | tf_op jit(solution)/shard_map/ppermute | solution.py:35
  685.4 73.3 %collective-permute-start.16 = (f32[256,1024]{1,0:T(8,128)}, f32[256,1024]{1,0:T(8,128)}, u32[]{:S(2)}, u32[]{:S(2)}) collective-permute-start(f32[256,1024]{1,0:T(8,128)} %copy.316), channel_id=1, source_target_pairs={{1,0},{4,1},{5,4},{8,5},{9,8},{12,9},{13,12},{3,2},{6,3},{7,6},{10... | collective-permute-start | bytes 3145736 | tf_op jit(solution)/shard_map/ppermute | solution.py:35
  (48 other events, 2244.4 us)
Sparse Core Ops, SparseCore 0:
  15.3 120.7 all-gather.5
  294.1 115.9 all-gather.7
where the time goes:
time: 856 us; the launch traced here: 845 us
  waiting for transfers between devices  323 us (38%)
  starting transfers between devices  134 us (16%)
  blocking collectives  116 us (14%)
  local copies, waits for them, and re-layouts  102 us (12%)
  matrix products  102 us (12%)
  other arithmetic  51.3 us (6%)
  between operations  16.1 us (2%)
    ppermute x32, waiting for transfers between devices, passed_along(): lax.ppermute(value, axis, [(source, source + steps) for source in range(f...  323 us
    ppermute x32, starting transfers between devices, passed_along(): lax.ppermute(value, axis, [(source, source + steps) for source in range(f...  134 us
    unnamed x1, blocking collectives  79.2 us
    slice x9, local copies, waits for them, and re-layouts, on_device(): value_terms[low_row:low_row + shard_rows]  28 us
    slice x9, local copies, waits for them, and re-layouts, on_device(): key_terms[low_row:low_row + shard_rows]  27.9 us
    dot_general x3, matrix products, ssd_block(): jnp.einsum('hts,shp->thp', gram_matrix[None] * decay_matrix, scaled_in, p...  22.4 us
    unnamed x100, local copies, waits for them, and re-layouts  21.6 us
  transfers between devices with their start and end apart: 34, of which 9 were waited for; matrix products, arithmetic and copies ran while one was open for 21% of the time, Pallas kernels for 0%

commit v1 on v0

v1 whole, which is shorter than its diff:
```python
import functools

import jax
import jax.numpy as jnp
from jax import lax
from jax.experimental import pallas as pl
from jax.experimental.pallas import tpu as pltpu
from jax.sharding import PartitionSpec as P

HP = 128
AD = 128
W = 2048
DI = 4096
LANES = 128
SLOTS = 16
EPSILON = 1e-05
LOG2E = 1.4426950408889634

HIGHEST = lax.Precision.HIGHEST
F32 = jnp.float32
BF16 = jnp.bfloat16
LINE = ("seq", "sub")
NN = (((1,), (0,)), ((), ()))
NT = (((1,), (1,)), ((), ()))
TN = (((0,), (0,)), ((), ()))


def mm(a, b, dims=NN, precision=None):
    return lax.dot_general(a, b, dims, precision=precision, preferred_element_type=F32)


def iota(shape, axis):
    return lax.broadcasted_iota(jnp.int32, shape, axis)


def call(body, grid, in_specs, out_specs, out_shape, scratch=(), flops=0, moved=0, exps=0):
    return pl.pallas_call(
        body,
        grid=grid,
        in_specs=in_specs,
        out_specs=out_specs,
        out_shape=out_shape,
        scratch_shapes=list(scratch),
        compiler_params=pltpu.CompilerParams(vmem_limit_bytes=56 * 2**20),
        cost_estimate=pl.CostEstimate(flops=flops // 1000, bytes_accessed=moved // 1000, transcendentals=exps // 1000),
    )


def whole(shape):
    return pl.BlockSpec(shape, lambda g: (0,) * len(shape))


def wide(rows, width):
    return pl.BlockSpec((rows, width), lambda g: (0, g))


def shaped(shape, dtype):
    return jax.ShapeDtypeStruct(shape, dtype)


def rolled(aux, first):
    return pltpu.roll(aux, lax.rem(LANES - first, LANES), 1)


def halves(wide_value):
    high = wide_value.astype(BF16)
    return high, (wide_value - high.astype(F32)).astype(BF16)


def mm_wide(wide_value, low, dims, swap=False):
    high, rest = halves(wide_value)
    if swap:
        return mm(low, high, dims) + mm(low, rest, dims)
    return mm(high, low, dims) + mm(rest, low, dims)


def decay_rows(last):
    high = last.astype(BF16)
    low = (last - high.astype(F32)).astype(BF16)
    row = iota((16, LANES), 0)
    return jnp.where(
        row == 0, high.astype(F32), jnp.where(row == 1, low.astype(F32), 0.0)
    ).astype(BF16)


def states_body(group, x_ref, b_ref, steps_ref, lr_ref, state_ref, own_ref, aux_ref, cum_ref):
    g = pl.program_id(0)
    rows = x_ref.shape[0]

    @pl.when(g == 0)
    def _():
        steps = steps_ref[...]
        logs = (-LOG2E * jnp.exp(lr_ref[...])) * steps
        less = -LOG2E * jnp.log(steps)
        r, c = iota((rows, rows), 0), iota((rows, rows), 1)
        lower = jnp.where(r >= c, 1.0, 0.0)
        eye = jnp.where(r == c, 1.0, 0.0)
        zero = jnp.zeros_like(logs)
        row = mm(logs, lower, NT, HIGHEST)
        cum_ref[:SLOTS] = row
        cum_ref[SLOTS:] = row + less
        logs_wide = jnp.concatenate([logs, zero, logs, logs, logs, logs, zero, zero], 0)
        plain_wide = jnp.concatenate([zero, steps, zero, steps, less, zero, zero, zero], 0)
        summed = mm(lower, logs_wide, NT, HIGHEST)
        plain = mm(eye, plain_wide, NT, HIGHEST)
        slot = iota((rows, LANES), 1) // SLOTS
        tail = jnp.exp2(summed[rows - 1 : rows] - summed)
        aux_ref[...] = jnp.where(
            slot == 2,
            jnp.exp2(summed),
            jnp.where(slot == 3, plain * tail, jnp.where(slot == 5, tail, summed + plain)),
        )

    aux = rolled(aux_ref[...], g * group)
    parts = []
    for k in range(group):
        weight = aux[:, 3 * SLOTS + k : 3 * SLOTS + k + 1]
        parts.append(x_ref[:, k * HP : (k + 1) * HP].astype(F32) * weight)
        last = aux[rows - 1 : rows, 2 * SLOTS + k : 2 * SLOTS + k + 1]
        state_ref[LANES:, k * HP : (k + 1) * HP] = decay_rows(jnp.broadcast_to(last, (1, LANES)))
    state = mm_wide(jnp.concatenate(parts, 1), b_ref[...], TN, True)
    state_ref[:LANES] = state.astype(BF16)
    own_ref[...] = state


def within_body(group, x_ref, b_ref, c_ref, aux_ref, cum_ref, y_ref, gram):
    g = pl.program_id(0)
    rows = x_ref.shape[0]

    @pl.when(g == 0)
    def _():
        r, c = iota((rows, rows), 0), iota((rows, rows), 1)
        gram[...] = jnp.where(r >= c, mm(c_ref[...], b_ref[...], NT), 0.0)

    aux = rolled(aux_ref[...], g * group)
    for k in range(group):
        row = cum_ref[pl.ds(SLOTS + g * group + k, 1), :]
        mix = (gram[...] * jnp.exp2(aux[:, k : k + 1] - row)).astype(BF16)
        y_ref[:, k * HP : (k + 1) * HP] = mm(mix, x_ref[:, k * HP : (k + 1) * HP])


def gate_body(
    group, groups, yin_ref, x_ref, gate_ref, mg_ref, c_ref, h_ref, aux_ref, skip_ref, gain_ref,
    y_ref, stat_ref, squares, crosses,
):
    g = pl.program_id(0)
    aux = rolled(aux_ref[...], g * group)
    carried = mm(c_ref[...], h_ref[...])
    square = jnp.zeros(squares.shape, F32)
    cross = jnp.zeros(squares.shape, F32)
    for k in range(group):
        at = slice(k * HP, (k + 1) * HP)
        grown = aux[:, 2 * SLOTS + k : 2 * SLOTS + k + 1]
        out = yin_ref[:, at] + carried[:, at] * grown
        y_ref[:, at] = out
        mixed = out + skip_ref[:, at] * x_ref[:, at].astype(F32)
        gate = gate_ref[:, at].astype(F32)
        gated = mixed * (gate / (1.0 + jnp.exp(-gate)))
        square += gated * gated
        cross += mg_ref[:, at].astype(F32) * gain_ref[:, at] * gated

    @pl.when(g == 0)
    def _():
        squares[...] = square
        crosses[...] = cross

    @pl.when(g > 0)
    def _():
        squares[...] += square
        crosses[...] += cross

    @pl.when(g == groups - 1)
    def _():
        ones = jnp.ones((8, LANES), F32)
        stat_ref[0:8] = mm(ones, squares[...], NT, HIGHEST)
        stat_ref[8:16] = mm(ones, crosses[...], NT, HIGHEST)


def pull_body(
    group, y_ref, x_ref, gate_ref, mg_ref, c_ref, aux_ref, sa_ref, sb_ref, skip_ref, gain_ref,
    dy_ref, pull_ref, own_ref, dgain_ref, dskip_ref, inverse, slope,
):
    g = pl.program_id(0)
    rows = x_ref.shape[0]

    @pl.when(g == 0)
    def _():
        r, c = iota((rows, rows), 0), iota((rows, rows), 1)
        eye = jnp.where(r == c, 1.0, 0.0)
        columns = mm(eye, sa_ref[...] + sb_ref[...], NT, HIGHEST)
        inv = lax.rsqrt(columns[:, 0:1] / DI + EPSILON)
        inverse[...] = jnp.broadcast_to(inv, inverse.shape)
        slope[...] = jnp.broadcast_to(inv * inv * inv * columns[:, 8:9] / DI, slope.shape)

    aux = rolled(aux_ref[...], g * group)
    parts = []
    for k in range(group):
        at = slice(k * HP, (k + 1) * HP)
        x = x_ref[:, at].astype(F32)
        gate = gate_ref[:, at].astype(F32)
        silu = gate / (1.0 + jnp.exp(-gate))
        gated = (y_ref[:, at] + skip_ref[:, at] * x) * silu
        scaled = mg_ref[:, at].astype(F32) * inverse[...]
        dgain_ref[:, at] = jnp.sum(scaled * gated, axis=0, keepdims=True)
        dy = (scaled * gain_ref[:, at] - gated * slope[...]) * silu
        dskip_ref[:, at] = jnp.sum(dy * x, axis=0, keepdims=True)
        dy_ref[:, at] = dy
        parts.append(dy * aux[:, 2 * SLOTS + k : 2 * SLOTS + k + 1])
        last = aux[rows - 1 : rows, 2 * SLOTS + k : 2 * SLOTS + k + 1]
        pull_ref[LANES:, at] = decay_rows(jnp.broadcast_to(last, (1, LANES)))
    pull = mm_wide(jnp.concatenate(parts, 1), c_ref[...], TN, True)
    pull_ref[:LANES] = pull.astype(BF16)
    own_ref[...] = pull


def within_back_body(
    group, groups, x_ref, dy_ref, y_ref, b_ref, c_ref, aux_ref, cum_ref, h_ref, skip_ref,
    dx_ref, dexit_ref, dentry_ref, cols_ref, gram, dgram,
):
    g = pl.program_id(0)
    rows = x_ref.shape[0]

    @pl.when(g == 0)
    def _():
        r, c = iota((rows, rows), 0), iota((rows, rows), 1)
        gram[...] = jnp.where(r <= c, mm(b_ref[...], c_ref[...], NT), 0.0)
        dgram[...] = jnp.zeros_like(dgram)
        dexit_ref[...] = jnp.zeros_like(dexit_ref)
        cols_ref[...] = jnp.zeros_like(cols_ref)

    aux = rolled(aux_ref[...], g * group)
    lane = iota((rows, LANES), 1)
    cols = cols_ref[...]
    total = dgram[...]
    parts = []
    for k in range(group):
        at = slice(k * HP, (k + 1) * HP)
        head = g * group + k
        row = cum_ref[pl.ds(head, 1), :]
        x_low = x_ref[:, at]
        dy = dy_ref[:, at]
        dy_low, dy_rest = halves(dy)
        decay = jnp.exp2(row - aux[:, 4 * SLOTS + k : 4 * SLOTS + k + 1])
        mix = (gram[...] * decay).astype(BF16)
        du = mm(mix, dy_low) + mm(mix, dy_rest)
        total = total + (mm(x_low, dy_low, NT) + mm(x_low, dy_rest, NT)) * decay
        into = jnp.sum(x_low.astype(F32) * du, axis=1, keepdims=True)
        out = jnp.sum(dy * y_ref[:, at], axis=1, keepdims=True)
        cols = jnp.where(lane == head, out - into, jnp.where(lane == SLOTS + head, into, cols))
        dx_ref[:, at] = du + skip_ref[:, at] * dy
        parts.append(dy * aux[:, 2 * SLOTS + k : 2 * SLOTS + k + 1])
    cols_ref[...] = cols
    dgram[...] = total
    dexit_ref[...] += mm_wide(jnp.concatenate(parts, 1), h_ref[...], NT)

    @pl.when(g == groups - 1)
    def _():
        r, c = iota((rows, rows), 0), iota((rows, rows), 1)
        kept = jnp.where(r <= c, total, 0.0)
        dentry_ref[...] = mm_wide(kept, c_ref[...], NN)
        dexit_ref[...] += mm_wide(kept, b_ref[...], TN)


def finish_body(
    group, groups, x_ref, dxin_ref, b_ref, f_ref, h_ref, aux_ref, cols_ref, din_ref, dout_ref, lr_ref,
    dx_ref, dsteps_ref, shared_ref, drate_ref, reach, inner,
):
    g = pl.program_id(0)
    rows = x_ref.shape[0]

    @pl.when(g == 0)
    def _():
        reach[...] = jnp.zeros_like(reach)
        inner[...] = jnp.zeros_like(inner)
        shared_ref[:rows] = din_ref[...]
        shared_ref[rows:] = dout_ref[...]

    aux = rolled(aux_ref[...], g * group)
    lane = iota((rows, LANES), 1)
    onward = f_ref[...]
    spread = mm(b_ref[...], onward)
    product = jnp.sum(onward.astype(F32) * h_ref[...].astype(F32), axis=0, keepdims=True)
    cols = reach[...]
    dots = inner[...]
    parts = []
    for k in range(group):
        at = slice(k * HP, (k + 1) * HP)
        head = g * group + k
        x = x_ref[:, at].astype(F32)
        weight = aux[:, 3 * SLOTS + k : 3 * SLOTS + k + 1]
        dx_ref[:, at] = (dxin_ref[:, at] + weight * spread[:, at]).astype(BF16)
        cols = jnp.where(lane == head, jnp.sum(x * spread[:, at], axis=1, keepdims=True), cols)
        dot = jnp.sum(product[:, at], axis=1, keepdims=True)
        dots = jnp.where(iota((1, LANES), 1) == head, dot, dots)
        parts.append(x * weight)
    reach[...] = cols
    inner[...] = dots
    shared_ref[:rows] += mm_wide(jnp.concatenate(parts, 1), onward, NT)

    @pl.when(g == groups - 1)
    def _():
        r, c = iota((rows, rows), 0), iota((rows, rows), 1)
        base = aux_ref[...]
        step = pltpu.roll(base, LANES - SLOTS, 1)
        grown = pltpu.roll(base, LANES - 2 * SLOTS, 1)
        tail = pltpu.roll(base, LANES - 5 * SLOTS, 1)
        edge = cols_ref[...]
        direct = pltpu.roll(edge, LANES - SLOTS, 1)
        live = lane < SLOTS
        passed = jnp.where(live, step * tail * cols, 0.0)
        change = jnp.where(live, edge, 0.0) - passed
        upper = jnp.where(r <= c, 1.0, 0.0)
        rate = -jnp.exp(lr_ref[...])
        dlog = (
            mm(upper, change, NN, HIGHEST)
            + jnp.sum(passed, axis=0, keepdims=True)
            + grown[rows - 1 : rows] * dots
        )
        dstep = jnp.where(live, direct / step + tail * cols + rate * dlog, 0.0)
        eye = jnp.where(r == c, 1.0, 0.0)
        dsteps_ref[...] = mm(dstep, eye, TN, HIGHEST)[:SLOTS]
        drate = jnp.sum(jnp.where(live, dlog * rate * step, 0.0), axis=0, keepdims=True)
        drate_ref[...] = jnp.broadcast_to(drate, drate_ref.shape)


def after(value, *others):
    return lax.optimization_barrier((value, *others))[0] if others else value


def chained(local, own_terms, reverse, on_send, on_held):
    chips = lax.axis_size("seq")
    first, second = (1, 0) if reverse else (0, 1)
    place = (lambda c: chips - 1 - c) if reverse else (lambda c: c)
    spot = place(lax.axis_index("seq"))
    joiner = lax.axis_index("sub") == second

    def split(terms):
        decay = terms[LANES : LANES + 1].astype(F32) + terms[LANES + 1 : LANES + 2].astype(F32)
        return terms[:LANES].astype(F32), decay

    near = lax.ppermute(local, LINE, [(2 * c + first, 2 * c + second) for c in range(chips)])
    near_terms, near_decay = split(near)
    own_decay = split(local)[1]
    total = own_decay * near_terms + own_terms
    decay = own_decay * near_decay
    held, reach = None, None
    half = 1
    while half < chips:
        final = 2 * half >= chips
        sent = total.astype(BF16)
        if not final:
            row = iota((16, local.shape[1]), 0)
            high, rest = halves(decay)
            rows = jnp.where(row == 0, high.astype(F32), jnp.where(row == 1, rest.astype(F32), 0.0))
            sent = jnp.concatenate([sent, rows.astype(BF16)], 0)
        sent = on_send(half, final, sent)
        got = None
        for k in range(half):
            pairs = [
                (2 * place(c + half - 1) + second, 2 * place(c + half + k) + second)
                for c in range(0, chips, 2 * half)
            ]
            came = lax.ppermute(sent, LINE, pairs)
            got = came if got is None else got + came
        upper = (spot // half) % 2 == 1
        if final:
            terms, brought = got.astype(F32), None
        else:
            terms, brought = split(got)
            total = decay * terms + total
            decay = jnp.where(upper, decay * brought, decay)
        held = terms if held is None else reach * terms + held
        if not final:
            reach = jnp.where(upper, brought if reach is None else reach * brought,
                              jnp.ones_like(brought) if reach is None else reach)
        half *= 2
    if held is None:
        held = jnp.zeros_like(own_terms)
    own = on_held(held)
    other = lax.ppermute(
        own.astype(BF16), LINE, [(2 * c + second, 2 * c + first) for c in range(chips)]
    )
    return jnp.where(joiner, (near_decay * held + near_terms).astype(BF16), other)


def mixer(x, gates, entry, exit_, steps, log_rates, skips, gains, mg, order):
    rows, width = x.shape
    heads = log_rates.shape[0]
    group = min(4, heads)
    groups = heads // group
    span = group * HP
    grid = (groups,)
    pad = SLOTS - heads
    steps_full = jnp.pad(steps, ((0, pad), (0, 0)), constant_values=1.0) if pad else steps
    rates_full = jnp.pad(log_rates, (0, pad)) if pad else log_rates
    rates_row = jnp.pad(rates_full, (0, LANES - SLOTS))[None]
    skip_row = jnp.repeat(skips, HP)[None]
    gain_row = gains[None]
    mega = rows * width

    state, state_own, aux, cum = call(
        functools.partial(states_body, group),
        grid,
        [wide(rows, span), whole((rows, HP)), whole((SLOTS, rows)), whole((SLOTS, 1))],
        [wide(LANES + 16, span), wide(LANES, span), whole((rows, LANES)), whole((2 * SLOTS, rows))],
        [
            shaped((LANES + 16, width), BF16),
            shaped((LANES, width), F32),
            shaped((rows, LANES), F32),
            shaped((2 * SLOTS, rows), F32),
        ],
        flops=2 * LANES * mega,
        moved=3 * mega,
    )(order.at_states(x), entry, steps_full, rates_full[:, None])
    within = call(
        functools.partial(within_body, group),
        grid,
        [
            wide(rows, span), whole((rows, HP)), whole((rows, HP)), whole((rows, LANES)),
            whole((2 * SLOTS, rows)),
        ],
        wide(rows, span),
        shaped((rows, width), F32),
        [pltpu.VMEM((rows, rows), F32)],
        flops=2 * rows * mega,
        moved=6 * mega,
        exps=rows * rows * heads,
    )(x, entry, exit_, aux, cum)
    within = order.after_within(within)
    start = chained(state, state_own, False, order.state_sent, order.state_held)
    y, stats = call(
        functools.partial(gate_body, group, groups),
        grid,
        [
            wide(rows, span), wide(rows, span), wide(rows, span), wide(rows, span),
            whole((rows, HP)), wide(LANES, span), whole((rows, LANES)), wide(1, span),
            wide(1, span),
        ],
        [wide(rows, span), whole((16, rows))],
        [shaped((rows, width), F32), shaped((16, rows), F32)],
        [pltpu.VMEM((rows, LANES), F32)] * 2,
        flops=2 * LANES * mega,
        moved=15 * mega,
        exps=mega,
    )(order.at_gate(within), x, gates, mg, exit_, start, aux, skip_row, gain_row)
    if lax.axis_size("head") == 2:
        stats_other = lax.ppermute(stats, "head", [(0, 1), (1, 0)])
    else:
        stats, stats_other = lax.psum(stats, "head"), jnp.zeros_like(stats)
    stats = order.at_pull(stats)
    dy, pull, pull_own, dgain, dskip = call(
        functools.partial(pull_body, group),
        grid,
        [
            wide(rows, span), wide(rows, span), wide(rows, span), wide(rows, span),
            whole((rows, HP)), whole((rows, LANES)), whole((16, rows)), whole((16, rows)),
            wide(1, span), wide(1, span),
        ],
        [wide(rows, span), wide(LANES + 16, span), wide(LANES, span), wide(1, span), wide(1, span)],
        [
            shaped((rows, width), F32),
            shaped((LANES + 16, width), BF16),
            shaped((LANES, width), F32),
            shaped((1, width), F32),
            shaped((1, width), F32),
        ],
        [pltpu.VMEM((rows, LANES), F32)] * 2,
        flops=2 * LANES * mega,
        moved=13 * mega,
        exps=mega,
    )(y, x, gates, mg, exit_, aux, stats, stats_other, skip_row, gain_row)
    dy, pull = order.at_within_back(dy), order.at_chain_back(pull)
    dx_part, dexit, dentry_part, cols = call(
        functools.partial(within_back_body, group, groups),
        grid,
        [
            wide(rows, span), wide(rows, span), wide(rows, span), whole((rows, HP)),
            whole((rows, HP)), whole((rows, LANES)), whole((2 * SLOTS, rows)), wide(LANES, span),
            wide(1, span),
        ],
        [wide(rows, span), whole((rows, HP)), whole((rows, HP)), whole((rows, LANES))],
        [
            shaped((rows, width), F32),
            shaped((rows, HP), F32),
            shaped((rows, HP), F32),
            shaped((rows, LANES), F32),
        ],
        [pltpu.VMEM((rows, rows), F32)] * 2,
        flops=5 * rows * mega,
        moved=13 * mega,
        exps=rows * rows * heads,
    )(x, dy, y, entry, exit_, aux, cum, start, skip_row)
    dx_part = order.after_within_back(dx_part)
    onward = chained(pull, pull_own, True, order.pull_sent, order.pull_held)
    dx, dsteps, shared, drate = call(
        functools.partial(finish_body, group, groups),
        grid,
        [
            wide(rows, span), wide(rows, span), whole((rows, HP)), wide(LANES, span),
            wide(LANES, span), whole((rows, LANES)), whole((rows, LANES)), whole((rows, HP)),
            whole((rows, HP)), whole((1, LANES)),
        ],
        [wide(rows, span), whole((SLOTS, rows)), whole((2 * rows, HP)), whole((8, LANES))],
        [
            shaped((rows, width), BF16),
            shaped((SLOTS, rows), F32),
            shaped((2 * rows, HP), F32),
            shaped((8, LANES), F32),
        ],
        [pltpu.VMEM((rows, LANES), F32), pltpu.VMEM((1, LANES), F32)],
        flops=4 * LANES * mega,
        moved=9 * mega,
    )(x, order.at_finish(dx_part), entry, onward, start, aux, cols, dentry_part, dexit, rates_row)

    drate = order.at_end(drate)
    if lax.axis_size("head") == 2:
        shared = shared + lax.ppermute(shared, "head", [(0, 1), (1, 0)])
    else:
        shared = lax.psum(shared, "head")
    shared = shared.astype(BF16)
    sums = order.at_sums(jnp.concatenate([dgain, dskip, drate[:1]], axis=1))
    count = lax.axis_size(LINE)
    step = 1
    while step < count:
        sums = sums + lax.ppermute(sums, LINE, [(i, i ^ step) for i in range(count)])
        step *= 2
    order.at_last(sums, shared)
    grad_gains = sums[0, :width]
    grad_skip = jnp.sum(sums[0, width : 2 * width].reshape(heads, HP), axis=1)
    grad_rates = sums[0, 2 * width : 2 * width + heads]
    return (
        dx, shared[:rows], shared[rows:], dsteps[:heads], grad_rates, grad_skip,
        grad_gains,
    )


def lane_block(ref, index):
    return ref[:, pl.ds(pl.multiple_of(index * AD, AD), AD)]


def deal_body(chips, *refs):
    ins, outs = refs[:4], refs[4:]
    chip, core = lax.axis_index("seq"), lax.axis_index("sub")
    for d in range(chips):
        for other in range(2):
            owner = 2 * (chip ^ d) + (core ^ other)
            for n in range(4):
                outs[d][other, n] = lane_block(ins[n], owner)


def gather_body(chips, *refs):
    near, far, outs = refs[:chips], refs[chips], refs[chips + 1 :]
    chip, core = lax.axis_index("seq"), lax.axis_index("sub")
    for d in range(chips):
        for other in range(2):
            owner = 2 * (chip ^ d) + (core ^ other)
            for n in range(3):
                block = far[d, n] if other else near[d][0, n]
                outs[n][:, pl.ds(pl.multiple_of(owner * AD, AD), AD)] = block


def attend_body(count, rows, *refs):
    chips = count // 2
    near, far, outs = refs[:chips], refs[chips], refs[chips + 1 : 2 * chips + 1]
    data, expo, dprob, tops, dkey, dval, dquery, sems = refs[2 * chips + 1 :]
    chip, core = lax.axis_index("seq"), lax.axis_index("sub")
    owner = lambda d, other: 2 * (chip ^ d) + (core ^ other)
    copies = []
    for d in range(chips):
        copies.append(
            pltpu.make_async_copy(near[d].at[0], data.at[owner(d, 0)], sems.at[2 * d])
        )
        copies.append(
            pltpu.make_async_copy(far.at[d], data.at[owner(d, 1)], sems.at[2 * d + 1])
        )
    for copy in copies:
        copy.start()
    dkey[...] = jnp.zeros_like(dkey)
    dval[...] = jnp.zeros_like(dval)
    for copy in copies:
        copy.wait()
    scale = AD ** (-0.5)
    span = 2 * rows
    k_at, q_at = iota((rows, span), 0), iota((rows, span), 1)

    def one_span(i, carry):
        query = data[pl.ds(2 * i, 2), 0].reshape(span, AD)
        grad = data[pl.ds(2 * i, 2), 3].reshape(span, AD)

        def soft(j, carry, shift):
            top, total = carry
            scores = mm(data[j, 1], query, NT)
            if shift is not None:
                scores = jnp.where(k_at + shift <= q_at, scores, -1e30)
            new_top = jnp.maximum(top, jnp.max(scores, axis=0, keepdims=True))
            e = jnp.exp2((scores - new_top) * (scale * LOG2E))
            expo[j] = e
            tops[j] = new_top
            kept = jnp.exp2((top - new_top) * (scale * LOG2E))
            return new_top, total * kept + jnp.sum(e, axis=0, keepdims=True)

        state = (jnp.full((1, span), -1e30, F32), jnp.zeros((1, span), F32))
        state = soft(2 * i, state, 0)
        state = soft(2 * i + 1, state, rows)
        top, total = lax.fori_loop(0, 2 * i, lambda j, s: soft(j, s, None), state)
        inverse = 1.0 / total

        def probs(j, delta):
            factor = jnp.exp2((tops[j] - top) * (scale * LOG2E)) * inverse
            p = expo[j] * factor
            low = p.astype(BF16)
            expo[j] = p
            dp = mm(data[j, 2], grad, NT)
            dprob[j] = dp
            dval[j] += mm(low, grad)
            return delta + jnp.sum(low.astype(F32) * dp, axis=0, keepdims=True)

        delta = lax.fori_loop(0, 2 * i + 2, probs, jnp.zeros((1, span), F32))
        dquery[...] = jnp.zeros_like(dquery)

        def back(j, carry):
            low = (expo[j] * (dprob[j] - delta) * scale).astype(BF16)
            dkey[j] += mm(low, query)
            dquery[...] += mm(low, data[j, 1], TN)
            return carry

        lax.fori_loop(0, 2 * i + 2, back, 0)
        data[2 * i, 3] = dquery[:rows].astype(BF16)
        data[2 * i + 1, 3] = dquery[rows:].astype(BF16)
        return carry

    lax.fori_loop(0, count // 2, one_span, 0)
    for d in range(chips):
        for other in range(2):
            at = owner(d, other)
            outs[d][other, 0] = data[at, 3]
            outs[d][other, 1] = dkey[at].astype(BF16)
            outs[d][other, 2] = dval[at].astype(BF16)


class Unordered:
    def state_sent(self, half, final, sent):
        return sent

    def pull_sent(self, half, final, sent):
        return sent

    def keep(self, value):
        return value

    at_states = after_within = after_within_back = at_gate = at_pull = at_chain_back = at_within_back = at_finish = at_sums = at_end = keep
    state_held = pull_held = keep

    def at_last(self, *values):
        pass


class ByHead(Unordered):
    def __init__(self, queries, keys, values, grad):
        self.inputs = (queries, keys, values, grad)
        self.rows, self.width = queries.shape
        self.count = lax.axis_size(LINE)
        self.chips = self.count // 2
        self.full = pl.BlockSpec((self.rows, self.width), lambda: (0, 0))
        self.dealt = call(
            functools.partial(deal_body, self.chips),
            (),
            [self.full] * 4,
            [self.pair(4)] * self.chips,
            [shaped((2, 4, self.rows, AD), BF16)] * self.chips,
            moved=16 * self.rows * self.width,
        )(*self.inputs)
        self.arrived = list(self.dealt)
        for d in range(1, self.chips):
            self.arrived[d] = self.swap(self.dealt[d], d)

    def pair(self, n):
        return pl.BlockSpec((2, n, self.rows, AD), lambda: (0, 0, 0, 0))

    def quad(self, n):
        return pl.BlockSpec((self.chips, n, self.rows, AD), lambda: (0, 0, 0, 0))

    def swap(self, a, d):
        return lax.ppermute(a, "seq", [(i, i ^ d) for i in range(self.chips)])

    def across(self, blocks):
        both = jnp.stack([b[1] for b in blocks])
        return lax.ppermute(both, "sub", [(0, 1), (1, 0)])

    def at_states(self, x):
        return after(x, self.dealt[0])

    def state_sent(self, half, final, sent):
        if half == 1:
            sent = after(sent, self.arrived[1], self.within)
        if final:
            sent = after(sent, *self.arrived[2:])
            self.far = self.across(self.arrived)
            self.attend(sent)
        return sent

    def state_held(self, held):
        return after(held, self.done[0])

    def after_within(self, within):
        self.within = within
        return within

    def at_pull(self, stats):
        return after(stats, self.returned[1])

    def at_chain_back(self, pull):
        return after(pull, self.returned[2])

    def after_within_back(self, dx):
        self.dx = dx
        return dx

    def pull_sent(self, half, final, sent):
        if half == 1:
            sent = after(sent, self.returned[3], self.dx)
        if final:
            self.back = self.across(self.returned)
            self.gather(sent)
        return sent

    def pull_held(self, held):
        return after(held, self.out[0])

    def attend(self, token):
        count, rows, width = self.count, self.rows, self.width
        near = [after(self.arrived[0], token)] + self.arrived[1:]
        self.done = call(
            functools.partial(attend_body, count, rows),
            (),
            [pl.BlockSpec(memory_space=pl.ANY)] * (self.chips + 1),
            [self.pair(3)] * self.chips,
            [shaped((2, 3, rows, AD), BF16)] * self.chips,
            [
                pltpu.VMEM((count, 4, rows, AD), BF16),
                pltpu.VMEM((count, rows, 2 * rows), F32),
                pltpu.VMEM((count, rows, 2 * rows), F32),
                pltpu.VMEM((count, 1, 2 * rows), F32),
                pltpu.VMEM((count, rows, AD), F32),
                pltpu.VMEM((count, rows, AD), F32),
                pltpu.VMEM((2 * rows, AD), F32),
                pltpu.SemaphoreType.DMA((count,)),
            ],
            flops=12 * AD * rows * rows * count * (count + 1) // 2,
            moved=14 * rows * width,
            exps=rows * rows * count * (count + 1) // 2,
        )(*near, self.far)
        self.returned = list(self.done)
        for d in range(1, self.chips):
            self.returned[d] = self.swap(self.done[d], d)

    def gather(self, token):
        self.out = call(
            functools.partial(gather_body, self.chips),
            (),
            [self.pair(3)] * self.chips + [self.quad(3)],
            [self.full] * 3,
            [shaped((self.rows, self.width), BF16)] * 3,
            moved=12 * self.rows * self.width,
        )(after(self.returned[0], token), *self.returned[1:], self.back)


def passed_along(value, axis, steps):
    count = lax.axis_size(axis)
    first, last = (max(0, -steps), min(count, count - steps))
    return lax.ppermute(value, axis, [(source, source + steps) for source in range(first, last)])


def window_grads(query_block, key_block, value_block, grad_block, query_pos, key_pos):
    score_scale = AD ** (-0.5)
    query_heads = query_block.reshape(query_block.shape[0], -1, AD)
    key_heads = key_block.reshape(key_block.shape[0], -1, AD)
    value_heads = value_block.reshape(value_block.shape[0], -1, AD)
    grad_heads = grad_block.reshape(grad_block.shape[0], -1, AD)
    scores = (
        jnp.einsum("thd,khd->htk", query_heads, key_heads, preferred_element_type=F32)
        * score_scale
    )
    gaps = query_pos[:, None] - key_pos[None, :]
    valid = (gaps >= 0) & (gaps < W) & (key_pos[None, :] >= 0)
    scores = jnp.where(valid[None], scores, -1e30)
    top_score = jnp.max(scores, axis=-1, keepdims=True)
    expos = jnp.exp(scores - top_score)
    probs = expos / jnp.sum(expos, axis=-1, keepdims=True)
    probs_low = probs.astype(BF16)
    attended = jnp.einsum("htk,khd->thd", probs_low, value_heads, preferred_element_type=F32)
    delta = jnp.sum(grad_heads.astype(F32) * attended, axis=-1).T
    dprobs = jnp.einsum("thd,khd->htk", grad_heads, value_heads, preferred_element_type=F32)
    dscores_low = (probs * (dprobs - delta[:, :, None]) * score_scale).astype(BF16)
    grad_query = jnp.einsum("htk,khd->thd", dscores_low, key_heads, preferred_element_type=F32)
    grad_key = jnp.einsum("htk,thd->khd", dscores_low, query_heads, preferred_element_type=F32)
    grad_value = jnp.einsum("htk,thd->khd", probs_low, grad_heads, preferred_element_type=F32)
    return (grad_query, grad_key, grad_value)


def attention_by_window(queries, key_rows, value_rows, attention_grad):
    shard_rows = queries.shape[0]
    reach_shards = W // shard_rows
    first_row = lax.axis_index(LINE) * shard_rows
    key_parts = []
    value_parts = []
    for shift_by in range(reach_shards, 0, -1):
        arrived = passed_along((key_rows, value_rows), LINE, shift_by)
        key_parts.append(arrived[0])
        value_parts.append(arrived[1])
    key_window = jnp.concatenate(key_parts + [key_rows], axis=0)
    value_window = jnp.concatenate(value_parts + [value_rows], axis=0)
    query_pos = first_row + jnp.arange(shard_rows, dtype=jnp.int32)
    key_pos = (
        first_row
        - reach_shards * shard_rows
        + jnp.arange((reach_shards + 1) * shard_rows, dtype=jnp.int32)
    )
    grad_query, grad_key, grad_value = window_grads(
        queries, key_window, value_window, attention_grad, query_pos, key_pos
    )
    key_terms = grad_key.reshape(grad_key.shape[0], -1)
    value_terms = grad_value.reshape(grad_value.shape[0], -1)
    key_total = key_terms[reach_shards * shard_rows :]
    value_total = value_terms[reach_shards * shard_rows :]
    for shift_by in range(1, reach_shards + 1):
        low_row = (reach_shards - shift_by) * shard_rows
        arrived = passed_along(
            (
                key_terms[low_row : low_row + shard_rows],
                value_terms[low_row : low_row + shard_rows],
            ),
            LINE,
            -shift_by,
        )
        key_total = key_total + arrived[0]
        value_total = value_total + arrived[1]
    return (
        grad_query.reshape(shard_rows, -1).astype(BF16),
        key_total.astype(BF16),
        value_total.astype(BF16),
    )


def on_device(
    ssm_inputs,
    gate_inputs,
    entry_coeffs,
    exit_coeffs,
    step_sizes,
    log_rates,
    skip_gains,
    norm_gains,
    mixer_grad,
    queries,
    key_rows,
    value_rows,
    attention_grad,
):
    count = lax.axis_size(LINE)
    by_head = queries.shape[1] == count * AD and queries.shape[0] * count <= W
    attention = (queries, key_rows, value_rows, attention_grad)
    order = ByHead(*attention) if by_head else Unordered()
    mixed = mixer(
        ssm_inputs, gate_inputs, entry_coeffs, exit_coeffs, step_sizes, log_rates, skip_gains,
        norm_gains, mixer_grad, order,
    )
    attended = order.out if by_head else attention_by_window(*attention)
    return (*mixed, *attended)


def solution(mesh):
    rows = ("parts", "seq", "sub")
    in_specs = (
        P(rows, "head"),
        P(rows, "head"),
        P(rows, None),
        P(rows, None),
        P("head", rows),
        P("head"),
        P("head"),
        P("head"),
        P(rows, "head"),
        P(rows, "head"),
        P(rows, "head"),
        P(rows, "head"),
        P(rows, "head"),
    )
    out_specs = (
        P(rows, "head"),
        P(rows, None),
        P(rows, None),
        P("head", rows),
        P(("parts", "head")),
        P(("parts", "head")),
        P(("parts", "head")),
        P(rows, "head"),
        P(rows, "head"),
        P(rows, "head"),
    )
    return jax.shard_map(
        on_device, mesh=mesh, in_specs=in_specs, out_specs=out_specs, check_vma=False
    )
```

time: 856 us -> 192 us (0.22); the launches traced: 845 us -> 191 us
  waiting for transfers between devices: 323 us -> 73.8 us
  blocking collectives: 116 us -> 0 us
  matrix products: 102 us -> 0 us
  starting transfers between devices: 134 us -> 34.8 us
  local copies, waits for them, and re-layouts: 102 us -> 5.17 us
  Pallas kernels: 0 us -> 66.9 us
  other arithmetic: 51.3 us -> 9.3 us
  between operations: 16.1 us -> 1.19 us
    ppermute x32 -> x23, waiting for transfers between devices: 323 us -> 73.8 us  [the longest x6 35.8 us: swap(): return lax.ppermute(a, 'seq', [(i, i ^ d) for i in range(self.chips)])]
    ppermute x32 -> x23, starting transfers between devices: 134 us -> 34.8 us  [the longest x6 19.2 us: swap(): return lax.ppermute(a, 'seq', [(i, i ^ d) for i in range(self.chips)])]
    dot_general x17 -> x0, matrix products: 89.1 us -> none  [the longest x3 22.4 us: ssd_block(): jnp.einsum('hts,shp->thp', gram_matrix[None] * decay_matrix, scaled_in, p...]
    unnamed x1 -> x0, blocking collectives: 79.2 us -> none
    pallas_call x0 -> x9, Pallas kernels: none -> 66.9 us  [the longest x1 21.3 us: attend(): call(functools.partial(attend_body, count, rows), (), [pl.BlockSpec(memor...]
    slice x22 -> x11, local copies, waits for them, and re-layouts: 61.4 us -> 2.08 us  [the longest x1 0.69 us: mixer(): sums = order.at_sums(jnp.concatenate([dgain, dskip, drate[:1]], axis=1))]
    psum x4 -> x0, blocking collectives: 36.8 us -> none  [the longest x1 14.7 us: on_device(): lax.psum((grads[5], skip_local, gain_local), ('seq', 'sub'))]
    unnamed x100 -> x34, local copies, waits for them, and re-layouts: 21.6 us -> 0.72 us
  transfers between devices with their start and end apart: 34 -> 23, of which waited for: 9 -> 13; matrix products, arithmetic and copies ran while one was open for 21% -> 4% of each run, Pallas kernels for 0% -> 26%
where the time goes in v1:
time: 192 us; the launch traced here: 191 us
  waiting for transfers between devices  73.8 us (38%)
  Pallas kernels  66.9 us (35%)
  starting transfers between devices  34.8 us (18%)
  other arithmetic  9.3 us (5%)
  local copies, waits for them, and re-layouts  5.17 us (3%)
    ppermute x6, waiting for transfers between devices, swap(): return lax.ppermute(a, 'seq', [(i, i ^ d) for i in range(self.chips)])  35.8 us
    ppermute x6, waiting for transfers between devices, chained(): came = lax.ppermute(sent, LINE, pairs)  26.9 us
    pallas_call x1, Pallas kernels, attend(): call(functools.partial(attend_body, count, rows), (), [pl.BlockSpec(memor...  21.3 us
    ppermute x6, starting transfers between devices, swap(): return lax.ppermute(a, 'seq', [(i, i ^ d) for i in range(self.chips)])  19.2 us
    pallas_call x1, Pallas kernels, mixer(): call(functools.partial(within_back_body, group, groups), grid, [wide(rows...  8.55 us
    pallas_call x1, Pallas kernels, mixer(): call(functools.partial(finish_body, group, groups), grid, [wide(rows, spa...  7.66 us
    ppermute x3, waiting for transfers between devices, mixer(): lax.ppermute(sums, LINE, [(i, i ^ step) for i in range(count)])  7.65 us
    pallas_call x1, Pallas kernels, mixer(): call(functools.partial(pull_body, group), grid, [wide(rows, span), wide(r...  6.6 us
  transfers between devices with their start and end apart: 23, of which 13 were waited for; matrix products, arithmetic and copies ran while one was open for 4% of the time, Pallas kernels for 26%

profile of v1, /device:TPU:0, one launch (start us, length us, event | category | flops | bytes accessed | tf_op | source)
XLA Modules:
  0.0 191.1 jit_solution(18041041210127687154)
XLA Ops:
  0.7 3.4 %shard_map.204 = (bf16[2,4,256,128]{3,2,1,0:T(8,128)(2,1)}, bf16[2,4,256,128]{3,2,1,0:T(8,128)(2,1)}, bf16[2,4,256,128]{3,2,1,0:T(8,128)(2,1)}, bf16[2,4,256,128]{3,2,1,0:T(8,128)(2,1)}) custom-call(bf16[256,1024]{1,0:T(8,128)(2,1)} %refs_0_.1, bf16[256,1024]{1,0:T(8,128)(2,1)} %refs_1_.1, bf16[256,1024]{1,0:T(8,128)(2,1)} %refs_2_.1, bf16[256,1024]{1,0:T(8,128)(2,1)} %refs_3_.1), custom_call_target="tpu_custom_call" | custom-call | bytes 4194 | tf_op jit(solution)/shard_map/pallas_call | solution.py:665
  4.7 5.3 %shard_map.205 = (bf16[144,2048]{1,0:T(8,128)(2,1)}, f32[128,2048]{1,0:T(8,128)}, f32[256,128]{1,0:T(8,128)}, f32[32,256]{1,0:T(8,128)}) custom-call(bf16[256,2048]{1,0:T(8,128)(2,1)} %x_ref.10, bf16[256,128]{1,0:T(8,128)(2,1)} %b_ref.7, f32[16,256]{1,0:T(8,128)} %steps_ref.1, f32[16,1]{1,0:T(8,128)} %copy.23.lr_ref), custom_call_target="tpu_custom_call" | custom-call | flops 134217 | bytes 1572 | tf_op jit(solution)/shard_map/pallas_call | solution.py:401
  10.0 2.4 %collective-permute-start = (bf16[144,2048]{1,0:T(8,128)(2,1)}, bf16[144,2048]{1,0:T(8,128)(2,1)S(1)}, u32[]{:S(2)}, u32[]{:S(2)}) collective-permute-start(bf16[144,2048]{1,0:T(8,128)(2,1)} %get-tuple-element.54), channel_id=1, source_target_pairs={{0,1},{4,5},{8,9},{12,13},{2,3},{6,7},{10,11},{14,15},{16,17},{20,... | collective-permute-start | bytes 1769480 | tf_op jit(solution)/shard_map/ppermute | solution.py:341
  12.4 2.5 %collective-permute-start.1 = (bf16[2,4,256,128]{3,2,1,0:T(8,128)(2,1)}, bf16[2,4,256,128]{3,2,1,0:T(8,128)(2,1)S(1)}, u32[]{:S(2)}, u32[]{:S(2)}) collective-permute-start(bf16[2,4,256,128]{3,2,1,0:T(8,128)(2,1)} %get-tuple-element.56), channel_id=1, source_target_pairs={{0,4},{4,0},{8,12},{12,8},{1,5},{5,1},{9,13},{13,9},{2,6},{6,2},{1... | collective-permute-start | bytes 1572872 | tf_op jit(solution)/shard_map/ppermute | solution.py:684
  14.9 2.6 %collective-permute-start.3 = (bf16[2,4,256,128]{3,2,1,0:T(8,128)(2,1)}, bf16[2,4,256,128]{3,2,1,0:T(8,128)(2,1)S(1)}, u32[]{:S(2)}, u32[]{:S(2)}) collective-permute-start(bf16[2,4,256,128]{3,2,1,0:T(8,128)(2,1)} %get-tuple-element.58), channel_id=1, source_target_pairs={{0,8},{4,12},{8,0},{12,4},{1,9},{5,13},{9,1},{13,5},{2,10},{6,14},... | collective-permute-start | bytes 1572872 | tf_op jit(solution)/shard_map/ppermute | solution.py:684
  17.5 5.0 %shard_map.206.yin_ref = f32[256,2048]{1,0:T(8,128)} custom-call(bf16[256,2048]{1,0:T(8,128)(2,1)} %x_ref.10, bf16[256,128]{1,0:T(8,128)(2,1)} %b_ref.7, bf16[256,128]{1,0:T(8,128)(2,1)} %c_ref.7, f32[256,128]{1,0:T(8,128)} %get-tuple-element.52.aux_ref, f32[32,256]{1,0:T(8,128)} %get-tuple-element.53.cum_ref), custom_call_target="tpu_custom_call" | custom-call | flops 268435 | bytes 3145 | tf_op jit(solution)/shard_map/pallas_call | solution.py:415
  23.7 13.1 %collective-permute-done.1.refs_1_ = bf16[2,4,256,128]{3,2,1,0:T(8,128)(2,1)S(1)} collective-permute-done((bf16[2,4,256,128]{3,2,1,0:T(8,128)(2,1)}, bf16[2,4,256,128]{3,2,1,0:T(8,128)(2,1)S(1)}, u32[]{:S(2)}, u32[]{:S(2)}) %collective-permute-start.1) | collective-permute-done | bytes 524320 | tf_op jit(solution)/shard_map/ppermute | solution.py:684
  37.6 13.8 %collective-permute-done.4.refs_3_ = bf16[2,4,256,128]{3,2,1,0:T(8,128)(2,1)S(1)} collective-permute-done((bf16[2,4,256,128]{3,2,1,0:T(8,128)(2,1)}, bf16[2,4,256,128]{3,2,1,0:T(8,128)(2,1)S(1)}, u32[]{:S(2)}, u32[]{:S(2)}) %collective-permute-start.4) | collective-permute-done | bytes 524320 | tf_op jit(solution)/shard_map/ppermute | solution.py:684
  51.3 1.9 %collective-permute-done.3.refs_2_ = bf16[2,4,256,128]{3,2,1,0:T(8,128)(2,1)S(1)} collective-permute-done((bf16[2,4,256,128]{3,2,1,0:T(8,128)(2,1)}, bf16[2,4,256,128]{3,2,1,0:T(8,128)(2,1)S(1)}, u32[]{:S(2)}, u32[]{:S(2)}) %collective-permute-start.3) | collective-permute-done | bytes 524320 | tf_op jit(solution)/shard_map/ppermute | solution.py:684
  57.5 21.3 %shard_map.207 = (bf16[2,3,256,128]{3,2,1,0:T(8,128)(2,1)}, bf16[2,3,256,128]{3,2,1,0:T(8,128)(2,1)}, bf16[2,3,256,128]{3,2,1,0:T(8,128)(2,1)}, bf16[2,3,256,128]{3,2,1,0:T(8,128)(2,1)}) custom-call(bf16[2,4,256,128]{3,2,1,0:T(8,128)(2,1)} %get-tuple-element.61.refs_0_, bf16[2,4,256,128]{3,2,1,0:T(8,128)(2,1)} %copy-done.3, ...), custom_call_target="tpu_custom_call" | custom-call | flops 3623878 | bytes 3670 | tf_op jit(solution)/shard_map/pallas_call | solution.py:733
  80.4 10.2 %collective-permute-start.9 = (bf16[2,3,256,128]{3,2,1,0:T(8,128)(2,1)}, bf16[2,3,256,128]{3,2,1,0:T(8,128)(2,1)S(1)}, u32[]{:S(2)}, u32[]{:S(2)}) collective-permute-start(bf16[2,3,256,128]{3,2,1,0:T(8,128)(2,1)} %get-tuple-element.66), channel_id=1, source_target_pairs={{0,4},{4,0},{8,12},{12,8},{1,5},{5,1},{9,13},{13,9},{2,6},{6,2},{1... | collective-permute-start | bytes 1179656 | tf_op jit(solution)/shard_map/ppermute | solution.py:684
  93.4 5.9 %shard_map.208 = (f32[256,2048]{1,0:T(8,128)}, f32[16,256]{1,0:T(8,128)}) custom-call(f32[256,2048]{1,0:T(8,128)} %shard_map.206.yin_ref, bf16[256,2048]{1,0:T(8,128)(2,1)} %x_ref.10, bf16[256,2048]{1,0:T(8,128)(2,1)} %gate_ref.3, bf16[256,2048]{1,0:T(8,128)(2,1)} %mg_ref.3, bf16[256,128]{1,0:T(8,128)(2,1)} %c_ref.7, bf16[128,2048]{1,0:T(8,128)(2,1)} %fusion.11.h_ref, ...), custom_call_target="tpu_custom_call" | custom-call | flops 134217 | bytes 7864 | tf_op jit(solution)/shard_map/pallas_call | solution.py:431
  99.4 1.5 collective-permute-start.10
  100.9 6.2 %collective-permute-done.9.refs_1_ = bf16[2,3,256,128]{3,2,1,0:T(8,128)(2,1)S(1)} collective-permute-done((bf16[2,3,256,128]{3,2,1,0:T(8,128)(2,1)}, bf16[2,3,256,128]{3,2,1,0:T(8,128)(2,1)S(1)}, u32[]{:S(2)}, u32[]{:S(2)}) %collective-permute-start.9) | collective-permute-done | bytes 393248 | tf_op jit(solution)/shard_map/ppermute | solution.py:684
  107.7 6.6 %shard_map.209 = (f32[256,2048]{1,0:T(8,128)}, bf16[144,2048]{1,0:T(8,128)(2,1)}, f32[128,2048]{1,0:T(8,128)}, f32[1,2048]{1,0:T(1,128)}, f32[1,2048]{1,0:T(1,128)}) custom-call(f32[256,2048]{1,0:T(8,128)} %get-tuple-element.64.y_ref, bf16[256,2048]{1,0:T(8,128)(2,1)} %x_ref.10, bf16[256,2048]{1,0:T(8,128)(2,1)} %gate_ref.3, bf16[256,2048]{1,0:T(8,128)(2,1)} %mg_ref.3, ...), custom_call_target="tpu_custom_call" | custom-call | flops 134217 | bytes 6815 | tf_op jit(solution)/shard_map/pallas_call | solution.py:451
  115.7 2.8 %collective-permute-start.13 = (bf16[2,3,256,128]{3,2,1,0:T(8,128)(2,1)S(1)}, bf16[2,3,256,128]{3,2,1,0:T(8,128)(2,1)S(1)}, u32[]{:S(2)}, u32[]{:S(2)}) collective-permute-start(bf16[2,3,256,128]{3,2,1,0:T(8,128)(2,1)S(1)} %copy-done.16), channel_id=1, source_target_pairs={{0,12},{4,8},{8,4},{12,0},{1,13},{5,9},{9,5},{13,1},{2,14},{6,10},... | collective-permute-start | bytes 1179656 | tf_op jit(solution)/shard_map/ppermute | solution.py:684
  118.4 8.5 %shard_map.210 = (f32[256,2048]{1,0:T(8,128)}, f32[256,128]{1,0:T(8,128)}, f32[256,128]{1,0:T(8,128)}, f32[256,128]{1,0:T(8,128)}) custom-call(bf16[256,2048]{1,0:T(8,128)(2,1)} %x_ref.10, f32[256,2048]{1,0:T(8,128)} %get-tuple-element.68.dy_ref, f32[256,2048]{1,0:T(8,128)} %get-tuple-element.64.y_ref, bf16[256,128]{1,0:T(8,128)(2,1)} %b_ref.7, ...), custom_call_target="tpu_custom_call" | custom-call | flops 671088 | bytes 6815 | tf_op jit(solution)/shard_map/pallas_call | solution.py:473
  130.6 13.5 %collective-permute-done.14 = bf16[144,2048]{1,0:T(8,128)(2,1)S(1)} collective-permute-done((bf16[144,2048]{1,0:T(8,128)(2,1)S(1)}, bf16[144,2048]{1,0:T(8,128)(2,1)S(1)}, u32[]{:S(2)}, u32[]{:S(2)}) %collective-permute-start.14) | collective-permute-done | bytes 589856 | tf_op jit(solution)/shard_map/ppermute | solution.py:363
  146.3 3.2 %shard_map.211 = (bf16[256,1024]{1,0:T(8,128)(2,1)}, bf16[256,1024]{1,0:T(8,128)(2,1)}, bf16[256,1024]{1,0:T(8,128)(2,1)}) custom-call(bf16[2,3,256,128]{3,2,1,0:T(8,128)(2,1)} %get-tuple-element.76.refs_0_, bf16[2,3,256,128]{3,2,1,0:T(8,128)(2,1)} %copy-done.7, bf16[2,3,256,128]{3,2,1,0:T(8,128)(2,1)} %copy-done.8, bf16[2,3,256,128]{3,2,1,0:T(8,128)(2,1)} %copy-done.9, ...), custom_call_target="tpu_custom_call" | custom-call | bytes 3145 | tf_op jit(solution)/shard_map/pallas_call | solution.py:758
  149.6 13.5 %collective-permute-done.16 = bf16[128,2048]{1,0:T(8,128)(2,1)} collective-permute-done((bf16[128,2048]{1,0:T(8,128)(2,1)S(1)}, bf16[128,2048]{1,0:T(8,128)(2,1)}, u32[]{:S(2)}, u32[]{:S(2)}) %collective-permute-start.16) | collective-permute-done | bytes 524320 | tf_op jit(solution)/shard_map/ppermute | solution.py:363
  168.2 7.7 %shard_map.212 = (bf16[256,2048]{1,0:T(8,128)(2,1)}, f32[16,256]{1,0:T(8,128)}, f32[512,128]{1,0:T(8,128)}, f32[8,128]{1,0:T(8,128)}) custom-call(bf16[256,2048]{1,0:T(8,128)(2,1)} %x_ref.10, f32[256,2048]{1,0:T(8,128)} %get-tuple-element.69.dxin_ref, bf16[256,128]{1,0:T(8,128)(2,1)} %b_ref.7, bf16[128,2048]{1,0:T(8,128)(2,1)} %fusion.10.f_ref, ...), custom_call_target="tpu_custom_call" | custom-call | flops 268435 | bytes 4718 | tf_op jit(solution)/shard_map/pallas_call | solution.py:495
  178.0 3.7 %collective-permute-done.21 = f32[1,4224]{1,0:T(1,128)S(1)} collective-permute-done((f32[1,4224]{1,0:T(1,128)S(1)}, f32[1,4224]{1,0:T(1,128)S(1)}, u32[]{:S(2)}, u32[]{:S(2)}) %collective-permute-start.21) | collective-permute-done | bytes 16928 | tf_op jit(solution)/shard_map/ppermute | solution.py:525
  181.8 1.6 collective-permute-start.19
  183.3 3.1 %collective-permute-done.22 = f32[1,4224]{1,0:T(1,128)S(1)} collective-permute-done((f32[1,4224]{1,0:T(1,128)S(1)}, f32[1,4224]{1,0:T(1,128)S(1)}, u32[]{:S(2)}, u32[]{:S(2)}) %collective-permute-start.22) | collective-permute-done | bytes 16928 | tf_op jit(solution)/shard_map/ppermute | solution.py:525
  (109 shorter events, 30.8 us)
Async XLA Ops:
  10.0 12.5 %collective-permute-start = (bf16[144,2048]{1,0:T(8,128)(2,1)}, bf16[144,2048]{1,0:T(8,128)(2,1)S(1)}, u32[]{:S(2)}, u32[]{:S(2)}) collective-permute-start(bf16[144,2048]{1,0:T(8,128)(2,1)} %get-tuple-element.54), channel_id=1, source_target_pairs={{0,1},{4,5},{8,9},{12,13},{2,3},{6,7},{10,11},{14,15},{16,17},{20,... | collective-permute-start | bytes 1769480 | tf_op jit(solution)/shard_map/ppermute | solution.py:341
  12.4 24.4 %collective-permute-start.1 = (bf16[2,4,256,128]{3,2,1,0:T(8,128)(2,1)}, bf16[2,4,256,128]{3,2,1,0:T(8,128)(2,1)S(1)}, u32[]{:S(2)}, u32[]{:S(2)}) collective-permute-start(bf16[2,4,256,128]{3,2,1,0:T(8,128)(2,1)} %get-tuple-element.56), channel_id=1, source_target_pairs={{0,4},{4,0},{8,12},{12,8},{1,5},{5,1},{9,13},{13,9},{2,6},{6,2},{1... | collective-permute-start | bytes 1572872 | tf_op jit(solution)/shard_map/ppermute | solution.py:684
  14.9 38.4 %collective-permute-start.3 = (bf16[2,4,256,128]{3,2,1,0:T(8,128)(2,1)}, bf16[2,4,256,128]{3,2,1,0:T(8,128)(2,1)S(1)}, u32[]{:S(2)}, u32[]{:S(2)}) collective-permute-start(bf16[2,4,256,128]{3,2,1,0:T(8,128)(2,1)} %get-tuple-element.58), channel_id=1, source_target_pairs={{0,8},{4,12},{8,0},{12,4},{1,9},{5,13},{9,1},{13,5},{2,10},{6,14},... | collective-permute-start | bytes 1572872 | tf_op jit(solution)/shard_map/ppermute | solution.py:684
  17.5 33.8 %collective-permute-start.4 = (bf16[2,4,256,128]{3,2,1,0:T(8,128)(2,1)}, bf16[2,4,256,128]{3,2,1,0:T(8,128)(2,1)S(1)}, u32[]{:S(2)}, u32[]{:S(2)}) collective-permute-start(bf16[2,4,256,128]{3,2,1,0:T(8,128)(2,1)} %get-tuple-element.59), channel_id=1, source_target_pairs={{0,12},{4,8},{8,4},{12,0},{1,13},{5,9},{9,5},{13,1},{2,14},{6,10},... | collective-permute-start | bytes 1572872 | tf_op jit(solution)/shard_map/ppermute | solution.py:684
  36.8 17.7 %collective-permute-start.2 = (bf16[144,2048]{1,0:T(8,128)(2,1)S(1)}, bf16[144,2048]{1,0:T(8,128)(2,1)S(1)}, u32[]{:S(2)}, u32[]{:S(2)}) collective-permute-start(bf16[144,2048]{1,0:T(8,128)(2,1)S(1)} %pad_maximum_fusion.2), channel_id=1, source_target_pairs={{1,5},{9,13},{3,7},{11,15},{17,21},{25,29},{19,23},{27,31}} | collective-permute-start | bytes 1769480 | tf_op jit(solution)/shard_map/ppermute | solution.py:363
  54.4 3.1 %collective-permute-start.7 = (bf16[4,4,256,128]{3,2,1,0:T(8,128)(2,1)}, bf16[4,4,256,128]{3,2,1,0:T(8,128)(2,1)}, u32[]{:S(2)}, u32[]{:S(2)}) collective-permute-start(bf16[4,4,256,128]{3,2,1,0:T(8,128)(2,1)} %pad_maximum_fusion), channel_id=1, source_target_pairs={{0,1},{1,0},{2,3},{3,2},{4,5},{5,4},{6,7},{7,6},{8,9},{9,8},{10,11... | collective-permute-start | bytes 3145736 | tf_op jit(solution)/shard_map/ppermute | solution.py:688
  54.8 24.0 %collective-permute-start.5 = (bf16[128,2048]{1,0:T(8,128)(2,1)S(1)}, bf16[128,2048]{1,0:T(8,128)(2,1)S(1)}, u32[]{:S(2)}, u32[]{:S(2)}) collective-permute-start(bf16[128,2048]{1,0:T(8,128)(2,1)S(1)} %fusion.3), channel_id=1, source_target_pairs={{5,9},{7,11},{21,25},{23,27}} | collective-permute-start | bytes 1572872 | tf_op jit(solution)/shard_map/ppermute | solution.py:363
  55.5 23.3 %collective-permute-start.6 = (bf16[128,2048]{1,0:T(8,128)(2,1)S(1)}, bf16[128,2048]{1,0:T(8,128)(2,1)S(1)}, u32[]{:S(2)}, u32[]{:S(2)}) collective-permute-start(bf16[128,2048]{1,0:T(8,128)(2,1)S(1)} %fusion.3), channel_id=1, source_target_pairs={{5,13},{7,15},{21,29},{23,31}} | collective-permute-start | bytes 1572872 | tf_op jit(solution)/shard_map/ppermute | solution.py:363
  79.1 12.6 %collective-permute-start.8 = (bf16[128,2048]{1,0:T(8,128)(2,1)S(1)}, bf16[128,2048]{1,0:T(8,128)(2,1)S(1)}, u32[]{:S(2)}, u32[]{:S(2)}) collective-permute-start(bf16[128,2048]{1,0:T(8,128)(2,1)S(1)} %convert_element_type.127), channel_id=1, source_target_pairs={{1,0},{5,4},{9,8},{13,12},{3,2},{7,6},{11,10},{15,14},{17,16},{21,... | collective-permute-start | bytes 1572872 | tf_op jit(solution)/shard_map/ppermute | solution.py:380
  80.4 26.7 %collective-permute-start.9 = (bf16[2,3,256,128]{3,2,1,0:T(8,128)(2,1)}, bf16[2,3,256,128]{3,2,1,0:T(8,128)(2,1)S(1)}, u32[]{:S(2)}, u32[]{:S(2)}) collective-permute-start(bf16[2,3,256,128]{3,2,1,0:T(8,128)(2,1)} %get-tuple-element.66), channel_id=1, source_target_pairs={{0,4},{4,0},{8,12},{12,8},{1,5},{5,1},{9,13},{13,9},{2,6},{6,2},{1... | collective-permute-start | bytes 1179656 | tf_op jit(solution)/shard_map/ppermute | solution.py:684
  90.6 23.8 %collective-permute-start.11 = (bf16[2,3,256,128]{3,2,1,0:T(8,128)(2,1)}, bf16[2,3,256,128]{3,2,1,0:T(8,128)(2,1)S(1)}, u32[]{:S(2)}, u32[]{:S(2)}) collective-permute-start(bf16[2,3,256,128]{3,2,1,0:T(8,128)(2,1)} %get-tuple-element.71), channel_id=1, source_target_pairs={{0,8},{4,12},{8,0},{12,4},{1,9},{5,13},{9,1},{13,5},{2,10},{6,14},... | collective-permute-start | bytes 1179656 | tf_op jit(solution)/shard_map/ppermute | solution.py:684
  99.4 7.7 %collective-permute-start.10 = (f32[16,256]{1,0:T(8,128)}, f32[16,256]{1,0:T(8,128)S(1)}, u32[]{:S(2)}, u32[]{:S(2)}) collective-permute-start(f32[16,256]{1,0:T(8,128)} %get-tuple-element.67.sa_ref), channel_id=1, source_target_pairs={{0,2},{2,0},{1,3},{3,1},{4,6},{6,4},{5,7},{7,5},{8,10},{10,8},{9,1... | collective-permute-start | bytes 49160 | tf_op jit(solution)/shard_map/ppermute | solution.py:447
  107.1 23.3 %copy-start.7 = (bf16[2,3,256,128]{3,2,1,0:T(8,128)(2,1)}, bf16[2,3,256,128]{3,2,1,0:T(8,128)(2,1)S(1)}, u32[]{:S(2)}) copy-start(bf16[2,3,256,128]{3,2,1,0:T(8,128)(2,1)S(1)} %collective-permute-done.9.refs_1_) | copy-start | bytes 1179652
  114.4 12.6 %collective-permute-start.12 = (bf16[144,2048]{1,0:T(8,128)(2,1)}, bf16[144,2048]{1,0:T(8,128)(2,1)S(1)}, u32[]{:S(2)}, u32[]{:S(2)}) collective-permute-start(bf16[144,2048]{1,0:T(8,128)(2,1)} %get-tuple-element.72), channel_id=1, source_target_pairs={{1,0},{5,4},{9,8},{13,12},{3,2},{7,6},{11,10},{15,14},{17,16},{21,... | collective-permute-start | bytes 1769480 | tf_op jit(solution)/shard_map/ppermute | solution.py:341
  115.7 13.3 %collective-permute-start.13 = (bf16[2,3,256,128]{3,2,1,0:T(8,128)(2,1)S(1)}, bf16[2,3,256,128]{3,2,1,0:T(8,128)(2,1)S(1)}, u32[]{:S(2)}, u32[]{:S(2)}) collective-permute-start(bf16[2,3,256,128]{3,2,1,0:T(8,128)(2,1)S(1)} %copy-done.16), channel_id=1, source_target_pairs={{0,12},{4,8},{8,4},{12,0},{1,13},{5,9},{9,5},{13,1},{2,14},{6,10},... | collective-permute-start | bytes 1179656 | tf_op jit(solution)/shard_map/ppermute | solution.py:684
  129.0 15.1 %collective-permute-start.14 = (bf16[144,2048]{1,0:T(8,128)(2,1)S(1)}, bf16[144,2048]{1,0:T(8,128)(2,1)S(1)}, u32[]{:S(2)}, u32[]{:S(2)}) collective-permute-start(bf16[144,2048]{1,0:T(8,128)(2,1)S(1)} %pad_maximum_fusion.3), channel_id=1, source_target_pairs={{12,8},{4,0},{14,10},{6,2},{28,24},{20,16},{30,26},{22,18}} | collective-permute-start | bytes 1769480 | tf_op jit(solution)/shard_map/ppermute | solution.py:363
  130.5 15.8 %collective-permute-start.17 = (bf16[4,3,256,128]{3,2,1,0:T(8,128)(2,1)S(1)}, bf16[4,3,256,128]{3,2,1,0:T(8,128)(2,1)}, u32[]{:S(2)}, u32[]{:S(2)}) collective-permute-start(bf16[4,3,256,128]{3,2,1,0:T(8,128)(2,1)S(1)} %pad_maximum_fusion.1), channel_id=1, source_target_pairs={{0,1},{1,0},{2,3},{3,2},{4,5},{5,4},{6,7},{7,6},{8,9},{9,8},{10,11... | collective-permute-start | bytes 2359304 | tf_op jit(solution)/shard_map/ppermute | solution.py:688
  144.3 5.3 %collective-permute-start.15 = (bf16[128,2048]{1,0:T(8,128)(2,1)S(1)}, bf16[128,2048]{1,0:T(8,128)(2,1)S(1)}, u32[]{:S(2)}, u32[]{:S(2)}) collective-permute-start(bf16[128,2048]{1,0:T(8,128)(2,1)S(1)} %fusion.7), channel_id=1, source_target_pairs={{8,4},{10,6},{24,20},{26,22}} | collective-permute-start | bytes 1572872 | tf_op jit(solution)/shard_map/ppermute | solution.py:363
  145.0 18.0 %collective-permute-start.16 = (bf16[128,2048]{1,0:T(8,128)(2,1)S(1)}, bf16[128,2048]{1,0:T(8,128)(2,1)}, u32[]{:S(2)}, u32[]{:S(2)}) collective-permute-start(bf16[128,2048]{1,0:T(8,128)(2,1)S(1)} %fusion.7), channel_id=1, source_target_pairs={{8,0},{10,2},{24,16},{26,18}} | collective-permute-start | bytes 1572872 | tf_op jit(solution)/shard_map/ppermute | solution.py:363
  164.4 2.8 %collective-permute-start.18 = (bf16[128,2048]{1,0:T(8,128)(2,1)S(1)}, bf16[128,2048]{1,0:T(8,128)(2,1)S(1)}, u32[]{:S(2)}, u32[]{:S(2)}) collective-permute-start(bf16[128,2048]{1,0:T(8,128)(2,1)S(1)} %convert_element_type.144), channel_id=1, source_target_pairs={{0,1},{4,5},{8,9},{12,13},{2,3},{6,7},{10,11},{14,15},{16,17},{20,... | collective-permute-start | bytes 1572872 | tf_op jit(solution)/shard_map/ppermute | solution.py:380
  176.6 1.3 collective-permute-start.20
  177.9 3.8 %collective-permute-start.21 = (f32[1,4224]{1,0:T(1,128)S(1)}, f32[1,4224]{1,0:T(1,128)S(1)}, u32[]{:S(2)}, u32[]{:S(2)}) collective-permute-start(f32[1,4224]{1,0:T(1,128)S(1)} %fusion.20), channel_id=1, source_target_pairs={{0,4},{1,5},{4,0},{5,1},{8,12},{9,13},{12,8},{13,9},{2,6},{3,7},{6... | collective-permute-start | bytes 50696 | tf_op jit(solution)/shard_map/ppermute | solution.py:525
  181.7 4.7 %collective-permute-start.22 = (f32[1,4224]{1,0:T(1,128)S(1)}, f32[1,4224]{1,0:T(1,128)S(1)}, u32[]{:S(2)}, u32[]{:S(2)}) collective-permute-start(f32[1,4224]{1,0:T(1,128)S(1)} %add.92), channel_id=1, source_target_pairs={{0,8},{1,9},{4,12},{5,13},{8,0},{9,1},{12,4},{13,5},{2,10},{3,11},... | collective-permute-start | bytes 50696 | tf_op jit(solution)/shard_map/ppermute | solution.py:525
  181.8 7.7 %collective-permute-start.19 = (f32[512,128]{1,0:T(8,128)}, f32[512,128]{1,0:T(8,128)S(1)}, u32[]{:S(2)}, u32[]{:S(2)}) collective-permute-start(f32[512,128]{1,0:T(8,128)} %get-tuple-element.83), channel_id=1, source_target_pairs={{0,2},{2,0},{1,3},{3,1},{4,6},{6,4},{5,7},{7,5},{8,10},{10,8},{9,1... | collective-permute-start | bytes 786440 | tf_op jit(solution)/shard_map/ppermute | solution.py:517
  (16 other events, 102.4 us)

commit v2 on v1

--- a/solution.py
+++ b/solution.py
@@ -386,10 +386,13 @@
 def mixer(x, gates, entry, exit_, steps, log_rates, skips, gains, mg, order):
     rows, width = x.shape
     heads = log_rates.shape[0]
-    group = min(4, heads)
+    group = min(8, heads)
     groups = heads // group
     span = group * HP
     grid = (groups,)
+    part = min(4, heads)
+    parts = heads // part
+    slim = part * HP
     pad = SLOTS - heads
     steps_full = jnp.pad(steps, ((0, pad), (0, 0)), constant_values=1.0) if pad else steps
     rates_full = jnp.pad(log_rates, (0, pad)) if pad else log_rates
@@ -471,14 +474,14 @@
     )(y, x, gates, mg, exit_, aux, stats, stats_other, skip_row, gain_row)
     dy, pull = order.at_within_back(dy), order.at_chain_back(pull)
     dx_part, dexit, dentry_part, cols = call(
-        functools.partial(within_back_body, group, groups),
-        grid,
+        functools.partial(within_back_body, part, parts),
+        (parts,),
         [
-            wide(rows, span), wide(rows, span), wide(rows, span), whole((rows, HP)),
-            whole((rows, HP)), whole((rows, LANES)), whole((2 * SLOTS, rows)), wide(LANES, span),
-            wide(1, span),
+            wide(rows, slim), wide(rows, slim), wide(rows, slim), whole((rows, HP)),
+            whole((rows, HP)), whole((rows, LANES)), whole((2 * SLOTS, rows)), wide(LANES, slim),
+            wide(1, slim),
         ],
-        [wide(rows, span), whole((rows, HP)), whole((rows, HP)), whole((rows, LANES))],
+        [wide(rows, slim), whole((rows, HP)), whole((rows, HP)), whole((rows, LANES))],
         [
             shaped((rows, width), F32),
             shaped((rows, HP), F32),
@@ -581,61 +584,59 @@
         copy.wait()
     scale = AD ** (-0.5)
     span = 2 * rows
-    k_at, q_at = iota((rows, span), 0), iota((rows, span), 1)
+    causal = iota((span, span), 0) <= iota((span, span), 1)
+    pair = lambda p, n: data[pl.ds(2 * p, 2), n].reshape(span, AD)
 
     def one_span(i, carry):
-        query = data[pl.ds(2 * i, 2), 0].reshape(span, AD)
-        grad = data[pl.ds(2 * i, 2), 3].reshape(span, AD)
-
-        def soft(j, carry, shift):
+        query, grad = pair(i, 0), pair(i, 3)
+
+        def soft(p, carry, diagonal=False):
             top, total = carry
-            scores = mm(data[j, 1], query, NT)
-            if shift is not None:
-                scores = jnp.where(k_at + shift <= q_at, scores, -1e30)
+            scores = mm(pair(p, 1), query, NT)
+            if diagonal:
+                scores = jnp.where(causal, scores, -1e30)
             new_top = jnp.maximum(top, jnp.max(scores, axis=0, keepdims=True))
             e = jnp.exp2((scores - new_top) * (scale * LOG2E))
-            expo[j] = e
-            tops[j] = new_top
+            expo[p] = e
+            tops[p] = new_top
             kept = jnp.exp2((top - new_top) * (scale * LOG2E))
             return new_top, total * kept + jnp.sum(e, axis=0, keepdims=True)
 
         state = (jnp.full((1, span), -1e30, F32), jnp.zeros((1, span), F32))
-        state = soft(2 * i, state, 0)
-        state = soft(2 * i + 1, state, rows)
-        top, total = lax.fori_loop(0, 2 * i, lambda j, s: soft(j, s, None), state)
+        top, total = lax.fori_loop(0, i, soft, soft(i, state, True))
         inverse = 1.0 / total
 
-        def probs(j, delta):
-            factor = jnp.exp2((tops[j] - top) * (scale * LOG2E)) * inverse
-            p = expo[j] * factor
-            low = p.astype(BF16)
-            expo[j] = p
-            dp = mm(data[j, 2], grad, NT)
-            dprob[j] = dp
-            dval[j] += mm(low, grad)
+        def probs(p, delta):
+            value = expo[p] * (jnp.exp2((tops[p] - top) * (scale * LOG2E)) * inverse)
+            low = value.astype(BF16)
+            expo[p] = value
+            dp = mm(pair(p, 2), grad, NT)
+            dprob[p] = dp
+            dval[p] += mm(low, grad)
             return delta + jnp.sum(low.astype(F32) * dp, axis=0, keepdims=True)
 
-        delta = lax.fori_loop(0, 2 * i + 2, probs, jnp.zeros((1, span), F32))
+        delta = lax.fori_loop(0, i + 1, probs, jnp.zeros((1, span), F32))
         dquery[...] = jnp.zeros_like(dquery)
 
-        def back(j, carry):
-            low = (expo[j] * (dprob[j] - delta) * scale).astype(BF16)
-            dkey[j] += mm(low, query)
-            dquery[...] += mm(low, data[j, 1], TN)
+        def back(p, carry):
+            low = (expo[p] * (dprob[p] - delta) * scale).astype(BF16)
+            dkey[p] += mm(low, query)
+            dquery[...] += mm(low, pair(p, 1), TN)
             return carry
 
-        lax.fori_loop(0, 2 * i + 2, back, 0)
+        lax.fori_loop(0, i + 1, back, 0)
         data[2 * i, 3] = dquery[:rows].astype(BF16)
         data[2 * i + 1, 3] = dquery[rows:].astype(BF16)
         return carry
 
     lax.fori_loop(0, count // 2, one_span, 0)
+    half = lambda ref, at: ref[at // 2, pl.ds(pl.multiple_of(at % 2 * rows, rows), rows)]
     for d in range(chips):
         for other in range(2):
             at = owner(d, other)
             outs[d][other, 0] = data[at, 3]
-            outs[d][other, 1] = dkey[at].astype(BF16)
-            outs[d][other, 2] = dval[at].astype(BF16)
+            outs[d][other, 1] = half(dkey, at).astype(BF16)
+            outs[d][other, 2] = half(dval, at).astype(BF16)
 
 
 class Unordered:
@@ -718,14 +719,19 @@
 
     def pull_sent(self, half, final, sent):
         if half == 1:
-            sent = after(sent, self.returned[3], self.dx)
+            self.returned[3] = self.swap(after(self.done[3], sent), 3)
         if final:
-            self.back = self.across(self.returned)
-            self.gather(sent)
+            sent = after(sent, self.dx)
         return sent
 
     def pull_held(self, held):
-        return after(held, self.out[0])
+        return after(held, self.returned[3])
+
+    def at_end(self, drate):
+        self.returned[1] = after(self.returned[1], drate)
+        self.back = self.across(self.returned)
+        self.gather(drate)
+        return drate
 
     def attend(self, token):
         count, rows, width = self.count, self.rows, self.width
@@ -738,11 +744,11 @@
             [shaped((2, 3, rows, AD), BF16)] * self.chips,
             [
                 pltpu.VMEM((count, 4, rows, AD), BF16),
-                pltpu.VMEM((count, rows, 2 * rows), F32),
-                pltpu.VMEM((count, rows, 2 * rows), F32),
-                pltpu.VMEM((count, 1, 2 * rows), F32),
-                pltpu.VMEM((count, rows, AD), F32),
-                pltpu.VMEM((count, rows, AD), F32),
+                pltpu.VMEM((self.chips, 2 * rows, 2 * rows), F32),
+                pltpu.VMEM((self.chips, 2 * rows, 2 * rows), F32),
+                pltpu.VMEM((self.chips, 1, 2 * rows), F32),
+                pltpu.VMEM((self.chips, 2 * rows, AD), F32),
+                pltpu.VMEM((self.chips, 2 * rows, AD), F32),
                 pltpu.VMEM((2 * rows, AD), F32),
                 pltpu.SemaphoreType.DMA((count,)),
             ],
@@ -751,7 +757,7 @@
             exps=rows * rows * count * (count + 1) // 2,
         )(*near, self.far)
         self.returned = list(self.done)
-        for d in range(1, self.chips):
+        for d in range(1, self.chips - 1):
             self.returned[d] = self.swap(self.done[d], d)
 
     def gather(self, token):

time: 192 us -> 187 us (0.974)
  Pallas kernels: 66.9 us -> 58.1 us
  starting transfers between devices: 34.8 us -> 39.9 us
  waiting for transfers between devices: 73.8 us -> 71.3 us
    ppermute x3, starting transfers between devices: 0.57 us -> 5.92 us  [mixer(): lax.ppermute(sums, LINE, [(i, i ^ step) for i in range(count)])]
    pallas_call x1, Pallas kernels: 21.3 us -> 17.4 us  [attend(): call(functools.partial(attend_body, count, rows), (), [pl.BlockSpec(memor...]
    ppermute x3, waiting for transfers between devices: 7.65 us -> 4.26 us  [mixer(): lax.ppermute(sums, LINE, [(i, i ^ step) for i in range(count)])]
    ppermute x2, waiting for transfers between devices: 0.01 us -> 3.26 us  [chained(): lax.ppermute(local, LINE, [(2 * c + first, 2 * c + second) for c in range...]
    ppermute x6, waiting for transfers between devices: 26.9 us -> 24.9 us  [chained(): came = lax.ppermute(sent, LINE, pairs)]
  transfers between devices with their start and end apart: 23 -> 23, of which waited for: 13 -> 13; matrix products, arithmetic and copies ran while one was open for 4% -> 5% of each run, Pallas kernels for 26% -> 22%
where the time goes in v2:
time: 187 us; the launch traced here: 186 us
  waiting for transfers between devices  71.3 us (38%)
  Pallas kernels  58.1 us (31%)
  starting transfers between devices  39.9 us (21%)
  other arithmetic  9.73 us (5%)
  local copies, waits for them, and re-layouts  6.1 us (3%)
    ppermute x6, waiting for transfers between devices, swap(): return lax.ppermute(a, 'seq', [(i, i ^ d) for i in range(self.chips)])  37.1 us
    ppermute x6, waiting for transfers between devices, chained(): came = lax.ppermute(sent, LINE, pairs)  24.9 us
    ppermute x6, starting transfers between devices, swap(): return lax.ppermute(a, 'seq', [(i, i ^ d) for i in range(self.chips)])  17.4 us
    pallas_call x1, Pallas kernels, attend(): call(functools.partial(attend_body, count, rows), (), [pl.BlockSpec(memor...  17.4 us
    pallas_call x1, Pallas kernels, mixer(): call(functools.partial(within_back_body, part, parts), (parts,), [wide(ro...  8.58 us
    ppermute x6, starting transfers between devices, chained(): came = lax.ppermute(sent, LINE, pairs)  6.29 us
    pallas_call x1, Pallas kernels, mixer(): call(functools.partial(finish_body, group, groups), grid, [wide(rows, spa...  6.26 us
    pallas_call x1, Pallas kernels, mixer(): call(functools.partial(pull_body, group), grid, [wide(rows, span), wide(r...  6.13 us
  transfers between devices with their start and end apart: 23, of which 13 were waited for; matrix products, arithmetic and copies ran while one was open for 5% of the time, Pallas kernels for 22%

profile of v2, /device:TPU:0, one launch (start us, length us, event | category | flops | bytes accessed | tf_op | source)
XLA Modules:
  0.0 186.3 jit_solution(13384790159723246314)
XLA Ops:
  0.7 3.4 %shard_map.204 = (bf16[2,4,256,128]{3,2,1,0:T(8,128)(2,1)}, bf16[2,4,256,128]{3,2,1,0:T(8,128)(2,1)}, bf16[2,4,256,128]{3,2,1,0:T(8,128)(2,1)}, bf16[2,4,256,128]{3,2,1,0:T(8,128)(2,1)}) custom-call(bf16[256,1024]{1,0:T(8,128)(2,1)} %refs_0_.1, bf16[256,1024]{1,0:T(8,128)(2,1)} %refs_1_.1, bf16[256,1024]{1,0:T(8,128)(2,1)} %refs_2_.1, bf16[256,1024]{1,0:T(8,128)(2,1)} %refs_3_.1), custom_call_target="tpu_custom_call" | custom-call | bytes 4194 | tf_op jit(solution)/shard_map/pallas_call | solution.py:666
  4.7 4.3 %shard_map.205 = (bf16[144,2048]{1,0:T(8,128)(2,1)}, f32[128,2048]{1,0:T(8,128)}, f32[256,128]{1,0:T(8,128)}, f32[32,256]{1,0:T(8,128)}) custom-call(bf16[256,2048]{1,0:T(8,128)(2,1)} %x_ref.10, bf16[256,128]{1,0:T(8,128)(2,1)} %b_ref.7, f32[16,256]{1,0:T(8,128)} %steps_ref.1, f32[16,1]{1,0:T(8,128)} %copy.23.lr_ref), custom_call_target="tpu_custom_call" | custom-call | flops 134217 | bytes 1572 | tf_op jit(solution)/shard_map/pallas_call | solution.py:404
  9.0 2.4 %collective-permute-start = (bf16[144,2048]{1,0:T(8,128)(2,1)}, bf16[144,2048]{1,0:T(8,128)(2,1)S(1)}, u32[]{:S(2)}, u32[]{:S(2)}) collective-permute-start(bf16[144,2048]{1,0:T(8,128)(2,1)} %get-tuple-element.56), channel_id=1, source_target_pairs={{0,1},{4,5},{8,9},{12,13},{2,3},{6,7},{10,11},{14,15},{16,17},{20,... | collective-permute-start | bytes 1769480 | tf_op jit(solution)/shard_map/ppermute | solution.py:341
  11.4 2.5 %collective-permute-start.1 = (bf16[2,4,256,128]{3,2,1,0:T(8,128)(2,1)}, bf16[2,4,256,128]{3,2,1,0:T(8,128)(2,1)S(1)}, u32[]{:S(2)}, u32[]{:S(2)}) collective-permute-start(bf16[2,4,256,128]{3,2,1,0:T(8,128)(2,1)} %get-tuple-element.58), channel_id=1, source_target_pairs={{0,4},{4,0},{8,12},{12,8},{1,5},{5,1},{9,13},{13,9},{2,6},{6,2},{1... | collective-permute-start | bytes 1572872 | tf_op jit(solution)/shard_map/ppermute | solution.py:685
  13.9 2.6 %collective-permute-start.3 = (bf16[2,4,256,128]{3,2,1,0:T(8,128)(2,1)}, bf16[2,4,256,128]{3,2,1,0:T(8,128)(2,1)S(1)}, u32[]{:S(2)}, u32[]{:S(2)}) collective-permute-start(bf16[2,4,256,128]{3,2,1,0:T(8,128)(2,1)} %get-tuple-element.60), channel_id=1, source_target_pairs={{0,8},{4,12},{8,0},{12,4},{1,9},{5,13},{9,1},{13,5},{2,10},{6,14},... | collective-permute-start | bytes 1572872 | tf_op jit(solution)/shard_map/ppermute | solution.py:685
  16.5 3.7 %shard_map.206.yin_ref = f32[256,2048]{1,0:T(8,128)} custom-call(bf16[256,2048]{1,0:T(8,128)(2,1)} %x_ref.10, bf16[256,128]{1,0:T(8,128)(2,1)} %b_ref.7, bf16[256,128]{1,0:T(8,128)(2,1)} %c_ref.7, f32[256,128]{1,0:T(8,128)} %get-tuple-element.54.aux_ref, f32[32,256]{1,0:T(8,128)} %get-tuple-element.55.cum_ref), custom_call_target="tpu_custom_call" | custom-call | flops 268435 | bytes 3145 | tf_op jit(solution)/shard_map/pallas_call | solution.py:418
  21.4 14.4 %collective-permute-done.1.refs_1_ = bf16[2,4,256,128]{3,2,1,0:T(8,128)(2,1)S(1)} collective-permute-done((bf16[2,4,256,128]{3,2,1,0:T(8,128)(2,1)}, bf16[2,4,256,128]{3,2,1,0:T(8,128)(2,1)S(1)}, u32[]{:S(2)}, u32[]{:S(2)}) %collective-permute-start.1) | collective-permute-done | bytes 524320 | tf_op jit(solution)/shard_map/ppermute | solution.py:685
  36.6 13.7 %collective-permute-done.4.refs_3_ = bf16[2,4,256,128]{3,2,1,0:T(8,128)(2,1)S(1)} collective-permute-done((bf16[2,4,256,128]{3,2,1,0:T(8,128)(2,1)}, bf16[2,4,256,128]{3,2,1,0:T(8,128)(2,1)S(1)}, u32[]{:S(2)}, u32[]{:S(2)}) %collective-permute-start.4) | collective-permute-done | bytes 524320 | tf_op jit(solution)/shard_map/ppermute | solution.py:685
  50.3 1.9 %collective-permute-done.3.refs_2_ = bf16[2,4,256,128]{3,2,1,0:T(8,128)(2,1)S(1)} collective-permute-done((bf16[2,4,256,128]{3,2,1,0:T(8,128)(2,1)}, bf16[2,4,256,128]{3,2,1,0:T(8,128)(2,1)S(1)}, u32[]{:S(2)}, u32[]{:S(2)}) %collective-permute-start.3) | collective-permute-done | bytes 524320 | tf_op jit(solution)/shard_map/ppermute | solution.py:685
  56.5 17.4 %shard_map.207 = (bf16[2,3,256,128]{3,2,1,0:T(8,128)(2,1)}, bf16[2,3,256,128]{3,2,1,0:T(8,128)(2,1)}, bf16[2,3,256,128]{3,2,1,0:T(8,128)(2,1)}, bf16[2,3,256,128]{3,2,1,0:T(8,128)(2,1)}) custom-call(bf16[2,4,256,128]{3,2,1,0:T(8,128)(2,1)} %get-tuple-element.63.refs_0_, bf16[2,4,256,128]{3,2,1,0:T(8,128)(2,1)} %copy-done.3, ...), custom_call_target="tpu_custom_call" | custom-call | flops 3623878 | bytes 3670 | tf_op jit(solution)/shard_map/pallas_call | solution.py:739
  75.5 10.2 %collective-permute-start.9 = (bf16[2,3,256,128]{3,2,1,0:T(8,128)(2,1)}, bf16[2,3,256,128]{3,2,1,0:T(8,128)(2,1)S(1)}, u32[]{:S(2)}, u32[]{:S(2)}) collective-permute-start(bf16[2,3,256,128]{3,2,1,0:T(8,128)(2,1)} %get-tuple-element.68), channel_id=1, source_target_pairs={{0,4},{4,0},{8,12},{12,8},{1,5},{5,1},{9,13},{13,9},{2,6},{6,2},{1... | collective-permute-start | bytes 1179656 | tf_op jit(solution)/shard_map/ppermute | solution.py:685
  88.5 5.1 %shard_map.208 = (f32[256,2048]{1,0:T(8,128)}, f32[16,256]{1,0:T(8,128)}) custom-call(f32[256,2048]{1,0:T(8,128)} %shard_map.206.yin_ref, bf16[256,2048]{1,0:T(8,128)(2,1)} %x_ref.10, bf16[256,2048]{1,0:T(8,128)(2,1)} %gate_ref.3, bf16[256,2048]{1,0:T(8,128)(2,1)} %mg_ref.3, bf16[256,128]{1,0:T(8,128)(2,1)} %c_ref.7, bf16[128,2048]{1,0:T(8,128)(2,1)} %fusion.11.h_ref, ...), custom_call_target="tpu_custom_call" | custom-call | flops 134217 | bytes 7864 | tf_op jit(solution)/shard_map/pallas_call | solution.py:434
  95.2 7.0 %collective-permute-done.9.refs_1_ = bf16[2,3,256,128]{3,2,1,0:T(8,128)(2,1)S(1)} collective-permute-done((bf16[2,3,256,128]{3,2,1,0:T(8,128)(2,1)}, bf16[2,3,256,128]{3,2,1,0:T(8,128)(2,1)S(1)}, u32[]{:S(2)}, u32[]{:S(2)}) %collective-permute-start.9) | collective-permute-done | bytes 393248 | tf_op jit(solution)/shard_map/ppermute | solution.py:685
  102.8 6.1 %shard_map.209 = (f32[256,2048]{1,0:T(8,128)}, bf16[144,2048]{1,0:T(8,128)(2,1)}, f32[128,2048]{1,0:T(8,128)}, f32[1,2048]{1,0:T(1,128)}, f32[1,2048]{1,0:T(1,128)}) custom-call(f32[256,2048]{1,0:T(8,128)} %get-tuple-element.66.y_ref, bf16[256,2048]{1,0:T(8,128)(2,1)} %x_ref.10, bf16[256,2048]{1,0:T(8,128)(2,1)} %gate_ref.3, bf16[256,2048]{1,0:T(8,128)(2,1)} %mg_ref.3, ...), custom_call_target="tpu_custom_call" | custom-call | flops 134217 | bytes 6815 | tf_op jit(solution)/shard_map/pallas_call | solution.py:454
  110.3 3.3 %collective-permute-done.12 = bf16[144,2048]{1,0:T(8,128)(2,1)S(1)} collective-permute-done((bf16[144,2048]{1,0:T(8,128)(2,1)}, bf16[144,2048]{1,0:T(8,128)(2,1)S(1)}, u32[]{:S(2)}, u32[]{:S(2)}) %collective-permute-start.12) | collective-permute-done | bytes 589856 | tf_op jit(solution)/shard_map/ppermute | solution.py:341
  117.4 8.6 %shard_map.210 = (f32[256,2048]{1,0:T(8,128)}, f32[256,128]{1,0:T(8,128)}, f32[256,128]{1,0:T(8,128)}, f32[256,128]{1,0:T(8,128)}) custom-call(bf16[256,2048]{1,0:T(8,128)(2,1)} %x_ref.10, f32[256,2048]{1,0:T(8,128)} %get-tuple-element.70.dy_ref, f32[256,2048]{1,0:T(8,128)} %get-tuple-element.66.y_ref, bf16[256,128]{1,0:T(8,128)(2,1)} %b_ref.7, ...), custom_call_target="tpu_custom_call" | custom-call | flops 671088 | bytes 6815 | tf_op jit(solution)/shard_map/pallas_call | solution.py:476
  126.0 1.7 collective-permute-done.13
  131.7 23.1 %collective-permute-done.15 = bf16[128,2048]{1,0:T(8,128)(2,1)} collective-permute-done((bf16[128,2048]{1,0:T(8,128)(2,1)S(1)}, bf16[128,2048]{1,0:T(8,128)(2,1)}, u32[]{:S(2)}, u32[]{:S(2)}) %collective-permute-start.15) | collective-permute-done | bytes 524320 | tf_op jit(solution)/shard_map/ppermute | solution.py:363
  156.4 2.1 %collective-permute-start.17 = (bf16[128,2048]{1,0:T(8,128)(2,1)S(1)}, bf16[128,2048]{1,0:T(8,128)(2,1)}, u32[]{:S(2)}, u32[]{:S(2)}) collective-permute-start(bf16[128,2048]{1,0:T(8,128)(2,1)S(1)} %convert_element_type.144), channel_id=1, source_target_pairs={{0,1},{4,5},{8,9},{12,13},{2,3},{6,7},{10,11},{14,15},{16,17},{20,... | collective-permute-start | bytes 1572872 | tf_op jit(solution)/shard_map/ppermute | solution.py:380
  160.4 6.3 %shard_map.211 = (bf16[256,2048]{1,0:T(8,128)(2,1)}, f32[16,256]{1,0:T(8,128)}, f32[512,128]{1,0:T(8,128)}, f32[8,128]{1,0:T(8,128)}) custom-call(bf16[256,2048]{1,0:T(8,128)(2,1)} %x_ref.10, f32[256,2048]{1,0:T(8,128)} %get-tuple-element.71.dxin_ref, bf16[256,128]{1,0:T(8,128)(2,1)} %b_ref.7, bf16[128,2048]{1,0:T(8,128)(2,1)} %fusion.10.f_ref, ...), custom_call_target="tpu_custom_call" | custom-call | flops 268435 | bytes 4718 | tf_op jit(solution)/shard_map/pallas_call | solution.py:498
  169.8 3.3 %collective-permute-start.20 = (f32[1,4224]{1,0:T(1,128)S(1)}, f32[1,4224]{1,0:T(1,128)S(1)}, u32[]{:S(2)}, u32[]{:S(2)}) collective-permute-start(f32[1,4224]{1,0:T(1,128)S(1)} %fusion.20), channel_id=1, source_target_pairs={{0,4},{1,5},{4,0},{5,1},{8,12},{9,13},{12,8},{13,9},{2,6},{3,7},{6... | collective-permute-start | bytes 50696 | tf_op jit(solution)/shard_map/ppermute | solution.py:528
  173.1 1.5 collective-permute-start.18
  176.1 3.4 %collective-permute-done.21 = f32[1,4224]{1,0:T(1,128)S(1)} collective-permute-done((f32[1,4224]{1,0:T(1,128)S(1)}, f32[1,4224]{1,0:T(1,128)S(1)}, u32[]{:S(2)}, u32[]{:S(2)}) %collective-permute-start.21) | collective-permute-done | bytes 16928 | tf_op jit(solution)/shard_map/ppermute | solution.py:528
  183.1 3.2 %shard_map.212 = (bf16[256,1024]{1,0:T(8,128)(2,1)}, bf16[256,1024]{1,0:T(8,128)(2,1)}, bf16[256,1024]{1,0:T(8,128)(2,1)}) custom-call(bf16[2,3,256,128]{3,2,1,0:T(8,128)(2,1)} %get-tuple-element.89.refs_0_, bf16[2,3,256,128]{3,2,1,0:T(8,128)(2,1)} %copy-done.7, bf16[2,3,256,128]{3,2,1,0:T(8,128)(2,1)} %copy-done.8, bf16[2,3,256,128]{3,2,1,0:T(8,128)(2,1)} %copy-done.9, ...), custom_call_target="tpu_custom_call" | custom-call | bytes 3145 | tf_op jit(solution)/shard_map/pallas_call | solution.py:764
  (111 shorter events, 33.9 us)
Async XLA Ops:
  9.0 11.2 %collective-permute-start = (bf16[144,2048]{1,0:T(8,128)(2,1)}, bf16[144,2048]{1,0:T(8,128)(2,1)S(1)}, u32[]{:S(2)}, u32[]{:S(2)}) collective-permute-start(bf16[144,2048]{1,0:T(8,128)(2,1)} %get-tuple-element.56), channel_id=1, source_target_pairs={{0,1},{4,5},{8,9},{12,13},{2,3},{6,7},{10,11},{14,15},{16,17},{20,... | collective-permute-start | bytes 1769480 | tf_op jit(solution)/shard_map/ppermute | solution.py:341
  11.4 24.4 %collective-permute-start.1 = (bf16[2,4,256,128]{3,2,1,0:T(8,128)(2,1)}, bf16[2,4,256,128]{3,2,1,0:T(8,128)(2,1)S(1)}, u32[]{:S(2)}, u32[]{:S(2)}) collective-permute-start(bf16[2,4,256,128]{3,2,1,0:T(8,128)(2,1)} %get-tuple-element.58), channel_id=1, source_target_pairs={{0,4},{4,0},{8,12},{12,8},{1,5},{5,1},{9,13},{13,9},{2,6},{6,2},{1... | collective-permute-start | bytes 1572872 | tf_op jit(solution)/shard_map/ppermute | solution.py:685
  13.9 38.4 %collective-permute-start.3 = (bf16[2,4,256,128]{3,2,1,0:T(8,128)(2,1)}, bf16[2,4,256,128]{3,2,1,0:T(8,128)(2,1)S(1)}, u32[]{:S(2)}, u32[]{:S(2)}) collective-permute-start(bf16[2,4,256,128]{3,2,1,0:T(8,128)(2,1)} %get-tuple-element.60), channel_id=1, source_target_pairs={{0,8},{4,12},{8,0},{12,4},{1,9},{5,13},{9,1},{13,5},{2,10},{6,14},... | collective-permute-start | bytes 1572872 | tf_op jit(solution)/shard_map/ppermute | solution.py:685
  16.5 33.8 %collective-permute-start.4 = (bf16[2,4,256,128]{3,2,1,0:T(8,128)(2,1)}, bf16[2,4,256,128]{3,2,1,0:T(8,128)(2,1)S(1)}, u32[]{:S(2)}, u32[]{:S(2)}) collective-permute-start(bf16[2,4,256,128]{3,2,1,0:T(8,128)(2,1)} %get-tuple-element.61), channel_id=1, source_target_pairs={{0,12},{4,8},{8,4},{12,0},{1,13},{5,9},{9,5},{13,1},{2,14},{6,10},... | collective-permute-start | bytes 1572872 | tf_op jit(solution)/shard_map/ppermute | solution.py:685
  35.8 17.7 %collective-permute-start.2 = (bf16[144,2048]{1,0:T(8,128)(2,1)S(1)}, bf16[144,2048]{1,0:T(8,128)(2,1)S(1)}, u32[]{:S(2)}, u32[]{:S(2)}) collective-permute-start(bf16[144,2048]{1,0:T(8,128)(2,1)S(1)} %pad_maximum_fusion.2), channel_id=1, source_target_pairs={{1,5},{9,13},{3,7},{11,15},{17,21},{25,29},{19,23},{27,31}} | collective-permute-start | bytes 1769480 | tf_op jit(solution)/shard_map/ppermute | solution.py:363
  53.4 3.1 %collective-permute-start.7 = (bf16[4,4,256,128]{3,2,1,0:T(8,128)(2,1)}, bf16[4,4,256,128]{3,2,1,0:T(8,128)(2,1)}, u32[]{:S(2)}, u32[]{:S(2)}) collective-permute-start(bf16[4,4,256,128]{3,2,1,0:T(8,128)(2,1)} %pad_maximum_fusion), channel_id=1, source_target_pairs={{0,1},{1,0},{2,3},{3,2},{4,5},{5,4},{6,7},{7,6},{8,9},{9,8},{10,11... | collective-permute-start | bytes 3145736 | tf_op jit(solution)/shard_map/ppermute | solution.py:689
  53.8 20.1 %collective-permute-start.5 = (bf16[128,2048]{1,0:T(8,128)(2,1)S(1)}, bf16[128,2048]{1,0:T(8,128)(2,1)S(1)}, u32[]{:S(2)}, u32[]{:S(2)}) collective-permute-start(bf16[128,2048]{1,0:T(8,128)(2,1)S(1)} %fusion.3), channel_id=1, source_target_pairs={{5,9},{7,11},{21,25},{23,27}} | collective-permute-start | bytes 1572872 | tf_op jit(solution)/shard_map/ppermute | solution.py:363
  54.5 19.4 %collective-permute-start.6 = (bf16[128,2048]{1,0:T(8,128)(2,1)S(1)}, bf16[128,2048]{1,0:T(8,128)(2,1)S(1)}, u32[]{:S(2)}, u32[]{:S(2)}) collective-permute-start(bf16[128,2048]{1,0:T(8,128)(2,1)S(1)} %fusion.3), channel_id=1, source_target_pairs={{5,13},{7,15},{21,29},{23,31}} | collective-permute-start | bytes 1572872 | tf_op jit(solution)/shard_map/ppermute | solution.py:363
  74.2 12.6 %collective-permute-start.8 = (bf16[128,2048]{1,0:T(8,128)(2,1)S(1)}, bf16[128,2048]{1,0:T(8,128)(2,1)S(1)}, u32[]{:S(2)}, u32[]{:S(2)}) collective-permute-start(bf16[128,2048]{1,0:T(8,128)(2,1)S(1)} %convert_element_type.127), channel_id=1, source_target_pairs={{1,0},{5,4},{9,8},{13,12},{3,2},{7,6},{11,10},{15,14},{17,16},{21,... | collective-permute-start | bytes 1572872 | tf_op jit(solution)/shard_map/ppermute | solution.py:380
  75.5 26.7 %collective-permute-start.9 = (bf16[2,3,256,128]{3,2,1,0:T(8,128)(2,1)}, bf16[2,3,256,128]{3,2,1,0:T(8,128)(2,1)S(1)}, u32[]{:S(2)}, u32[]{:S(2)}) collective-permute-start(bf16[2,3,256,128]{3,2,1,0:T(8,128)(2,1)} %get-tuple-element.68), channel_id=1, source_target_pairs={{0,4},{4,0},{8,12},{12,8},{1,5},{5,1},{9,13},{13,9},{2,6},{6,2},{1... | collective-permute-start | bytes 1179656 | tf_op jit(solution)/shard_map/ppermute | solution.py:685
  85.7 23.3 %collective-permute-start.11 = (bf16[2,3,256,128]{3,2,1,0:T(8,128)(2,1)}, bf16[2,3,256,128]{3,2,1,0:T(8,128)(2,1)S(1)}, u32[]{:S(2)}, u32[]{:S(2)}) collective-permute-start(bf16[2,3,256,128]{3,2,1,0:T(8,128)(2,1)} %get-tuple-element.73), channel_id=1, source_target_pairs={{0,8},{4,12},{8,0},{12,4},{1,9},{5,13},{9,1},{13,5},{2,10},{6,14},... | collective-permute-start | bytes 1179656 | tf_op jit(solution)/shard_map/ppermute | solution.py:685
  93.6 8.6 %collective-permute-start.10 = (f32[16,256]{1,0:T(8,128)}, f32[16,256]{1,0:T(8,128)S(1)}, u32[]{:S(2)}, u32[]{:S(2)}) collective-permute-start(f32[16,256]{1,0:T(8,128)} %get-tuple-element.69.sa_ref), channel_id=1, source_target_pairs={{0,2},{2,0},{1,3},{3,1},{4,6},{6,4},{5,7},{7,5},{8,10},{10,8},{9,1... | collective-permute-start | bytes 49160 | tf_op jit(solution)/shard_map/ppermute | solution.py:450
  102.2 72.5 %copy-start.7 = (bf16[2,3,256,128]{3,2,1,0:T(8,128)(2,1)}, bf16[2,3,256,128]{3,2,1,0:T(8,128)(2,1)S(1)}, u32[]{:S(2)}) copy-start(bf16[2,3,256,128]{3,2,1,0:T(8,128)(2,1)S(1)} %collective-permute-done.9.refs_1_) | copy-start | bytes 1179652
  109.0 4.6 %collective-permute-start.12 = (bf16[144,2048]{1,0:T(8,128)(2,1)}, bf16[144,2048]{1,0:T(8,128)(2,1)S(1)}, u32[]{:S(2)}, u32[]{:S(2)}) collective-permute-start(bf16[144,2048]{1,0:T(8,128)(2,1)} %get-tuple-element.74), channel_id=1, source_target_pairs={{1,0},{5,4},{9,8},{13,12},{3,2},{7,6},{11,10},{15,14},{17,16},{21,... | collective-permute-start | bytes 1769480 | tf_op jit(solution)/shard_map/ppermute | solution.py:341
  115.9 11.8 %collective-permute-start.13 = (bf16[144,2048]{1,0:T(8,128)(2,1)S(1)}, bf16[144,2048]{1,0:T(8,128)(2,1)S(1)}, u32[]{:S(2)}, u32[]{:S(2)}) collective-permute-start(bf16[144,2048]{1,0:T(8,128)(2,1)S(1)} %pad_maximum_fusion.3), channel_id=1, source_target_pairs={{12,8},{4,0},{14,10},{6,2},{28,24},{20,16},{30,26},{22,18}} | collective-permute-start | bytes 1769480 | tf_op jit(solution)/shard_map/ppermute | solution.py:363
  127.9 3.8 %collective-permute-start.14 = (bf16[128,2048]{1,0:T(8,128)(2,1)S(1)}, bf16[128,2048]{1,0:T(8,128)(2,1)}, u32[]{:S(2)}, u32[]{:S(2)}) collective-permute-start(bf16[128,2048]{1,0:T(8,128)(2,1)S(1)} %fusion.7), channel_id=1, source_target_pairs={{8,4},{10,6},{24,20},{26,22}} | collective-permute-start | bytes 1572872 | tf_op jit(solution)/shard_map/ppermute | solution.py:363
  129.4 25.5 %collective-permute-start.15 = (bf16[128,2048]{1,0:T(8,128)(2,1)S(1)}, bf16[128,2048]{1,0:T(8,128)(2,1)}, u32[]{:S(2)}, u32[]{:S(2)}) collective-permute-start(bf16[128,2048]{1,0:T(8,128)(2,1)S(1)} %fusion.7), channel_id=1, source_target_pairs={{8,0},{10,2},{24,16},{26,18}} | collective-permute-start | bytes 1572872 | tf_op jit(solution)/shard_map/ppermute | solution.py:363
  130.7 25.6 %collective-permute-start.16 = (bf16[2,3,256,128]{3,2,1,0:T(8,128)(2,1)}, bf16[2,3,256,128]{3,2,1,0:T(8,128)(2,1)S(1)}, u32[]{:S(2)}, u32[]{:S(2)}) collective-permute-start(bf16[2,3,256,128]{3,2,1,0:T(8,128)(2,1)} %get-tuple-element.78), channel_id=1, source_target_pairs={{0,12},{4,8},{8,4},{12,0},{1,13},{5,9},{9,5},{13,1},{2,14},{6,10},... | collective-permute-start | bytes 1179656 | tf_op jit(solution)/shard_map/ppermute | solution.py:685
  156.4 2.9 %collective-permute-start.17 = (bf16[128,2048]{1,0:T(8,128)(2,1)S(1)}, bf16[128,2048]{1,0:T(8,128)(2,1)}, u32[]{:S(2)}, u32[]{:S(2)}) collective-permute-start(bf16[128,2048]{1,0:T(8,128)(2,1)S(1)} %convert_element_type.144), channel_id=1, source_target_pairs={{0,1},{4,5},{8,9},{12,13},{2,3},{6,7},{10,11},{14,15},{16,17},{20,... | collective-permute-start | bytes 1572872 | tf_op jit(solution)/shard_map/ppermute | solution.py:380
  167.4 2.3 %collective-permute-start.19 = (f32[1,4224]{1,0:T(1,128)S(1)}, f32[1,4224]{1,0:T(1,128)S(1)}, u32[]{:S(2)}, u32[]{:S(2)}) collective-permute-start(f32[1,4224]{1,0:T(1,128)S(1)} %pad_maximum_fusion.4), channel_id=1, source_target_pairs={{0,1},{1,0},{4,5},{5,4},{8,9},{9,8},{12,13},{13,12},{2,3},{3,2},{6... | collective-permute-start | bytes 50696 | tf_op jit(solution)/shard_map/ppermute | solution.py:528
  169.8 5.0 %collective-permute-start.20 = (f32[1,4224]{1,0:T(1,128)S(1)}, f32[1,4224]{1,0:T(1,128)S(1)}, u32[]{:S(2)}, u32[]{:S(2)}) collective-permute-start(f32[1,4224]{1,0:T(1,128)S(1)} %fusion.20), channel_id=1, source_target_pairs={{0,4},{1,5},{4,0},{5,1},{8,12},{9,13},{12,8},{13,9},{2,6},{3,7},{6... | collective-permute-start | bytes 50696 | tf_op jit(solution)/shard_map/ppermute | solution.py:528
  173.1 8.3 %collective-permute-start.18 = (f32[512,128]{1,0:T(8,128)S(1)}, f32[512,128]{1,0:T(8,128)S(1)}, u32[]{:S(2)}, u32[]{:S(2)}) collective-permute-start(f32[512,128]{1,0:T(8,128)S(1)} %copy-done.11), channel_id=1, source_target_pairs={{0,2},{2,0},{1,3},{3,1},{4,6},{6,4},{5,7},{7,5},{8,10},{10,8},{9,1... | collective-permute-start | bytes 786440 | tf_op jit(solution)/shard_map/ppermute | solution.py:520
  174.8 4.7 %collective-permute-start.21 = (f32[1,4224]{1,0:T(1,128)S(1)}, f32[1,4224]{1,0:T(1,128)S(1)}, u32[]{:S(2)}, u32[]{:S(2)}) collective-permute-start(f32[1,4224]{1,0:T(1,128)S(1)} %add.92), channel_id=1, source_target_pairs={{0,8},{1,9},{4,12},{5,13},{8,0},{9,1},{12,4},{13,5},{2,10},{3,11},... | collective-permute-start | bytes 50696 | tf_op jit(solution)/shard_map/ppermute | solution.py:528
  176.1 6.1 %collective-permute-start.22 = (bf16[4,3,256,128]{3,2,1,0:T(8,128)(2,1)S(1)}, bf16[4,3,256,128]{3,2,1,0:T(8,128)(2,1)S(1)}, u32[]{:S(2)}, u32[]{:S(2)}) collective-permute-start(bf16[4,3,256,128]{3,2,1,0:T(8,128)(2,1)S(1)} %pad_maximum_fusion.1), channel_id=1, source_target_pairs={{0,1},{1,0},{2,3},{3,2},{4,5},{5,4},{6,7},{7,6},{8,9},{9,8},{10,11... | collective-permute-start | bytes 2359304 | tf_op jit(solution)/shard_map/ppermute | solution.py:689
  (17 other events, 174.3 us)
